TPU v7x, 256 devices: a whole 4x4x8 slice. The times are simulated.
256 devices in a mesh: gx: 32 (over z, x_hi, core), gy: 8 (over x_lo, y).
Axes of the slice: x: 4 (x_hi: 2, x_lo: 2; x = x_hi * 2 + x_lo), y: 4, z: 8, core: 2. Of those that a mesh axis runs over, the one named last changes fastest.
Arguments:
- field_in: bfloat16 [3, 64, 256, 128], P(None, 'gx', 'gy'), may hold values from -6 to 6
- conv_first: bfloat16 [32, 27, 3], replicated, may hold values from -0.625 to 0.625
- bias_first: float32 [32], replicated, may hold values from -3 to 3
- conv_second: bfloat16 [32, 27, 32], replicated, may hold values from -0.21875 to 0.21875
- cotangent: bfloat16 [32, 64, 256, 128], P(None, 'gx', 'gy'), may hold values from -6 to 6
- mask_first: int32 [32, 64, 256, 128], P(None, 'gx', 'gy'), may hold values 0 or 1
- mask_second: int32 [32, 64, 256, 128], P(None, 'gx', 'gy'), may hold values 0 or 1
Outputs:
- input_grad: float32 [3, 64, 256, 128], P(None, 'gx', 'gy')
- grad_conv_first: float32 [32, 27, 3], P('gx')
- grad_conv_second: float32 [32, 27, 32], P('gx')
All inputs are finite; a program needn't handle non-finite values. No bound on the sum of `mask_first` or of `mask_second` on one device may be relied on, other than what follows from the above.
Results may differ from a plain program's by a relative error of at most 0.004.
Values may be sent and summed in bfloat16 or wider, within the bound.
A program may use at most 64 MiB of HBM per device.

v0:
```python
import math

import jax
import jax.numpy as jnp
from jax import lax
from jax.sharding import PartitionSpec as P

leak_slope = 0.01


def extended(cells, sides, width):
    for axis, dim in sides:
        count = lax.axis_size(axis)
        head = lax.slice_in_dim(cells, 0, width, axis=dim)
        tail = lax.slice_in_dim(cells, cells.shape[dim] - width, cells.shape[dim], axis=dim)
        cells = jnp.concatenate(
            [
                lax.ppermute(tail, axis, [(i, (i + 1) % count) for i in range(count)]),
                cells,
                lax.ppermute(head, axis, [((i + 1) % count, i) for i in range(count)]),
            ],
            axis=dim,
        )
    return cells


def mask_factor(mask_values):
    return jnp.where(mask_values == 1, 1.0, leak_slope).astype(jnp.float32)


def leaky_relu(values):
    return jnp.where(values >= 0, values, leak_slope * values)


def shifted_copies(padded):
    return [jnp.roll(padded, 1 - tap_z, axis=3) for tap_z in range(3)]


def tap_block(rolled, shift_x, size_x, size_y):
    return jnp.stack(
        [
            rolled[tap_z][:, shift_x : shift_x + size_x, tap_y : tap_y + size_y, :]
            for tap_y in range(3)
            for tap_z in range(3)
        ],
        axis=0,
    )


def correlate(padded, weights, size_x, size_y):
    rolled = shifted_copies(padded)
    running = None
    for tap_x in range(3):
        stacked = tap_block(rolled, tap_x, size_x, size_y)
        product = jnp.einsum(
            "tcxyz,otc->oxyz",
            stacked,
            weights[:, 9 * tap_x : 9 * tap_x + 9, :],
            preferred_element_type=jnp.float32,
        )
        running = product if running is None else running + product
    return running


def weight_terms(grad_vals, padded):
    size_x = grad_vals.shape[1]
    size_y = grad_vals.shape[2]
    rolled = shifted_copies(padded)
    columns = [
        jnp.einsum(
            "oxyz,tcxyz->otc",
            grad_vals,
            tap_block(rolled, tap_x, size_x, size_y),
            preferred_element_type=jnp.float32,
        )
        for tap_x in range(3)
    ]
    return jnp.concatenate(columns, axis=1)


def on_device(field_in, conv_first, bias_first, conv_second, cotangent, mask_first, mask_second):
    size_x = field_in.shape[1]
    size_y = field_in.shape[2]
    bias_col = bias_first[:, None, None, None]
    near_in = extended(field_in, (("gx", 1), ("gy", 2)), 1)
    pre_act = correlate(near_in, conv_first, size_x, size_y) + bias_col
    hidden_local = leaky_relu(pre_act).astype(jnp.bfloat16)
    hidden_pad = extended(hidden_local, (("gx", 1), ("gy", 2)), 1)
    cot_masked = (cotangent.astype(jnp.float32) * mask_factor(mask_second)).astype(jnp.bfloat16)
    cot_pad = extended(cot_masked, (("gx", 1), ("gy", 2)), 1)
    second_t = conv_second[:, ::-1, :].transpose(2, 1, 0)
    grad_hidden = correlate(cot_pad, second_t, size_x, size_y)
    grad_masked = (grad_hidden * mask_factor(mask_first)).astype(jnp.bfloat16)
    first_t = conv_first[:, ::-1, :].transpose(2, 1, 0)
    grad_pad = extended(grad_masked, (("gx", 1), ("gy", 2)), 1)
    input_grad = correlate(grad_pad, first_t, size_x, size_y)
    first_terms = weight_terms(grad_masked, near_in)
    second_terms = weight_terms(cot_masked, hidden_pad)
    norm_scale = 1.0 / math.sqrt(
        size_x * lax.axis_size("gx") * size_y * lax.axis_size("gy") * field_in.shape[3]
    )
    summed = lax.psum((first_terms, second_terms), ("gx", "gy"))
    width_part = first_terms.shape[0] // lax.axis_size("gx")
    offset = lax.axis_index("gx") * width_part
    grad_first = lax.dynamic_slice_in_dim(summed[0], offset, width_part, 0)
    grad_second = lax.dynamic_slice_in_dim(summed[1], offset, width_part, 0)
    return (input_grad, grad_first * norm_scale, grad_second * norm_scale)


def solution(mesh):
    placed = (
        P(None, "gx", "gy", None),
        P(),
        P(),
        P(),
        P(None, "gx", "gy", None),
        P(None, "gx", "gy", None),
        P(None, "gx", "gy", None),
    )
    return jax.shard_map(
        on_device,
        mesh=mesh,
        in_specs=placed,
        out_specs=(P(None, "gx", "gy", None), P("gx", None, None), P("gx", None, None)),
        check_vma=False,
    )
```

profile of v0, /device:TPU:1, one launch (start us, length us, event | category | flops | bytes accessed | tf_op | source)
XLA Modules:
  0.0 465.7 jit_solution(726651102578416439)
XLA Ops:
  7.2 0.8 fusion.152
  8.0 4.1 collective-permute-start.8
  12.1 2.3 multiply_convert_fusion
  14.5 2.4 collective-permute-done.9
  16.9 2.8 collective-permute-start.11
  19.8 0.8 fusion.148
  20.6 3.1 collective-permute-start.1
  26.0 0.7 copy.1540
  26.7 0.7 copy.1541
  28.9 0.7 copy.1545
  30.3 0.7 copy.1547
  31.0 0.7 copy.1530
  31.7 0.7 copy.1531
  32.4 0.7 copy.1532
  33.9 0.7 copy.1535
  34.6 0.7 copy.1536
  35.3 0.7 copy.1537
  36.0 0.7 copy.1538
  36.7 1.5 stack.479
  38.3 1.4 convolution_bitcast_fusion
  39.8 4.0 stack.469
  43.9 1.4 convolution_bitcast_fusion.1
  45.3 4.4 stack.459
  49.7 2.2 fusion.19
  52.0 0.9 fusion.146
  52.8 4.7 %collective-permute-start.13 = (bf16[32,1,32,128]{3,0,2,1:T(8,128)(2,1)}, bf16[32,1,32,128]{3,0,2,1:T(8,128)(2,1)S(1)}, u32[]{:S(2)}, u32[]{:S(2)}) collective-permute-start(bf16[32,1,32,128]{3,0,2,1:T(8,128)(2,1)} %get-tuple-element.145), channel_id=1, source_target_pairs={{8,0},{16,8},{24,16},{32,24},{40,32},{48,40},{56,48},{64,56},{72,6... | collective-permute-start | bytes 786440 | tf_op jit(solution)/shard_map/ppermute | solution.py:20
  57.6 1.8 copy.1520
  59.3 0.9 reverse_bitcast_fusion
  60.3 3.0 collective-permute-start.3
  63.4 0.9 collective-permute-done.12
  64.3 1.3 pad_maximum_fusion.29
  65.7 3.0 collective-permute-start.15
  75.2 0.7 fusion.92
  77.8 1.0 fusion.7
  78.7 1.0 fusion.4
  80.0 1.5 fusion.18
  81.5 0.8 fusion.147
  83.8 8.8 %collective-permute-start.5 = (bf16[32,1,32,128]{3,0,2,1:T(8,128)(2,1)}, bf16[32,1,32,128]{3,0,2,1:T(8,128)(2,1)S(1)}, u32[]{:S(2)}, u32[]{:S(2)}) collective-permute-start(bf16[32,1,32,128]{3,0,2,1:T(8,128)(2,1)} %get-tuple-element.149), channel_id=1, source_target_pairs={{8,0},{16,8},{24,16},{32,24},{40,32},{48,40},{56,48},{64,56},{72,6... | collective-permute-start | bytes 786440 | tf_op jit(solution)/shard_map/ppermute | solution.py:20
  93.1 82.1 %psum.14 = f32[32,27,3]{0,1,2:T(8,128)S(1)} all-reduce(f32[32,27,3]{0,1,2:T(8,128)S(1)} %pad_maximum_fusion.26), channel_id=1, replica_groups=mesh['gx'=32,'gy'=8] {'gx','gy'}, use_global_device_ids=true, to_apply=%region_0.1 | all-reduce | flops 2592 | bytes 20736 | tf_op jit(solution)/shard_map/psum | solution.py:102
  176.0 1.2 pad_maximum_fusion.2
  178.4 1.3 pad_maximum_fusion.5
  180.6 1.0 fusion.45
  182.0 0.9 fusion.42
  183.3 1.1 fusion.40
  184.4 0.8 fusion.36
  185.4 0.8 fusion.35
  186.2 0.8 fusion.34
  187.2 0.8 fusion.32
  188.1 3.5 convolution_bitcast_fusion.4
  191.5 3.5 convolution_bitcast_fusion.5
  195.0 3.5 convolution_bitcast_fusion.6
  198.5 0.8 pad_maximum_fusion.18
  199.3 1.4 collective-permute-start.7
  201.1 244.1 %all-reduce.2.cloned.1.call-done = f32[32,27,32]{2,0,1:T(8,128)} async-done(((f32[32,27,32]{2,0,1:T(8,128)}), f32[32,27,32]{2,0,1:T(8,128)}) %all-reduce.2.cloned.1.call-update) | async-done | bytes 110608 | tf_op jit(solution)/shard_map/psum | solution.py:102
  445.1 1.5 dynamic-slice_multiply_fusion.1
  449.8 0.9 fusion.72
  450.9 1.1 fusion.70
  452.0 0.8 fusion.66
  453.0 0.8 fusion.65
  453.8 0.8 fusion.64
  454.8 0.8 fusion.62
  455.6 0.8 fusion.137
  456.4 0.8 fusion.138
  457.2 0.8 fusion.139
  (147 shorter events, 24.3 us)
Async XLA Ops:
  7.2 9.7 %copy-start.2 = (bf16[3,2,32,128]{3,2,1,0:T(8,128)(2,1)S(1)}, bf16[3,2,32,128]{3,2,1,0:T(8,128)(2,1)}, u32[]{:S(2)}) copy-start(bf16[3,2,32,128]{3,2,1,0:T(8,128)(2,1)} %param.7) | copy-start | bytes 147460
  7.2 438.0 %all-reduce.2.cloned.1.call-start = ((), (), s32[]{:S(2)}) async-start(), calls=%async_computation | async-start | bytes 884736 | tf_op jit(solution)/shard_map/psum | solution.py:102
  8.0 6.5 %collective-permute-start.8 = (bf16[3,1,32,128]{3,2,1,0:T(8,128)(2,1)S(1)}, bf16[3,1,32,128]{3,2,1,0:T(8,128)(2,1)S(1)}, u32[]{:S(2)}, u32[]{:S(2)}) collective-permute-start(bf16[3,1,32,128]{3,2,1,0:T(8,128)(2,1)S(1)} %get-tuple-element.189), channel_id=1, source_target_pairs={{0,8},{8,16},{16,24},{24,32},{32,40},{40,48},{48,56},{56,64},{64,7... | collective-permute-start | bytes 73736 | tf_op jit(solution)/shard_map/ppermute | solution.py:18
  12.1 4.8 %collective-permute-start.9 = (bf16[3,1,32,128]{3,2,1,0:T(8,128)(2,1)S(1)}, bf16[3,1,32,128]{3,2,1,0:T(8,128)(2,1)S(1)}, u32[]{:S(2)}, u32[]{:S(2)}) collective-permute-start(bf16[3,1,32,128]{3,2,1,0:T(8,128)(2,1)S(1)} %get-tuple-element.188), channel_id=1, source_target_pairs={{8,0},{16,8},{24,16},{32,24},{40,32},{48,40},{56,48},{64,56},{72,6... | collective-permute-start | bytes 73736 | tf_op jit(solution)/shard_map/ppermute | solution.py:20
  14.5 9.4 %copy-start.3 = (bf16[32,27,3]{1,0,2:T(8,128)(2,1)S(1)}, bf16[32,27,3]{1,0,2:T(8,128)(2,1)}, u32[]{:S(2)}) copy-start(bf16[32,27,3]{1,0,2:T(8,128)(2,1)} %param.8) | copy-start | bytes 15556
  16.9 7.3 %collective-permute-start.11 = (bf16[3,4,1,128]{3,2,1,0:T(2,128)(2,1)S(1)}, bf16[3,4,1,128]{3,2,1,0:T(2,128)(2,1)S(1)}, u32[]{:S(2)}, u32[]{:S(2)}) collective-permute-start(bf16[3,4,1,128]{3,2,1,0:T(2,128)(2,1)S(1)} %get-tuple-element.184), channel_id=1, source_target_pairs={{1,0},{2,1},{3,2},{4,3},{5,4},{6,5},{7,6},{0,7},{9,8},{10,9},{11,1... | collective-permute-start | bytes 9224 | tf_op jit(solution)/shard_map/ppermute | solution.py:20
  19.8 4.6 collective-permute-start.10
  20.6 39.7 %collective-permute-start.1 = (bf16[32,1,32,128]{3,0,2,1:T(8,128)(2,1)}, bf16[32,1,32,128]{3,0,2,1:T(8,128)(2,1)S(1)}, u32[]{:S(2)}, u32[]{:S(2)}) collective-permute-start(bf16[32,1,32,128]{3,0,2,1:T(8,128)(2,1)} %get-tuple-element.151), channel_id=1, source_target_pairs={{8,0},{16,8},{24,16},{32,24},{40,32},{48,40},{56,48},{64,56},{72,6... | collective-permute-start | bytes 786440 | tf_op jit(solution)/shard_map/ppermute | solution.py:20
  23.7 36.6 %collective-permute-start = (bf16[32,1,32,128]{3,0,2,1:T(8,128)(2,1)}, bf16[32,1,32,128]{3,0,2,1:T(8,128)(2,1)S(1)}, u32[]{:S(2)}, u32[]{:S(2)}) collective-permute-start(bf16[32,1,32,128]{3,0,2,1:T(8,128)(2,1)} %get-tuple-element.150), channel_id=1, source_target_pairs={{0,8},{8,16},{16,24},{24,32},{32,40},{40,48},{48,56},{56,64},{64,7... | collective-permute-start | bytes 786440 | tf_op jit(solution)/shard_map/ppermute | solution.py:18
  38.2 1.5 copy-start.4
  38.2 1.5 copy-start.5
  38.3 1.5 copy-start.6
  38.3 1.5 copy-start.7
  38.3 1.5 copy-start.8
  43.8 1.5 copy-start.9
  43.8 1.5 copy-start.10
  43.8 1.5 copy-start.11
  43.8 1.5 copy-start.12
  43.8 1.5 copy-start.13
  43.8 1.5 copy-start.14
  43.8 1.5 copy-start.15
  45.3 4.4 copy-start.16
  52.8 10.5 %collective-permute-start.13 = (bf16[32,1,32,128]{3,0,2,1:T(8,128)(2,1)}, bf16[32,1,32,128]{3,0,2,1:T(8,128)(2,1)S(1)}, u32[]{:S(2)}, u32[]{:S(2)}) collective-permute-start(bf16[32,1,32,128]{3,0,2,1:T(8,128)(2,1)} %get-tuple-element.145), channel_id=1, source_target_pairs={{8,0},{16,8},{24,16},{32,24},{40,32},{48,40},{56,48},{64,56},{72,6... | collective-permute-start | bytes 786440 | tf_op jit(solution)/shard_map/ppermute | solution.py:20
  57.6 6.8 %collective-permute-start.12 = (bf16[32,1,32,128]{3,0,2,1:T(8,128)(2,1)}, bf16[32,1,32,128]{3,0,2,1:T(8,128)(2,1)}, u32[]{:S(2)}, u32[]{:S(2)}) collective-permute-start(bf16[32,1,32,128]{3,0,2,1:T(8,128)(2,1)} %get-tuple-element.144), channel_id=1, source_target_pairs={{0,8},{8,16},{16,24},{24,32},{32,40},{40,48},{48,56},{56,64},{64,7... | collective-permute-start | bytes 786440 | tf_op jit(solution)/shard_map/ppermute | solution.py:18
  60.3 8.3 %collective-permute-start.3 = (bf16[32,4,1,128]{3,0,2,1:T(8,128)(2,1)S(1)}, bf16[32,4,1,128]{3,0,2,1:T(8,128)(2,1)S(1)}, u32[]{:S(2)}, u32[]{:S(2)}) collective-permute-start(bf16[32,4,1,128]{3,0,2,1:T(8,128)(2,1)S(1)} %get-tuple-element.141), channel_id=1, source_target_pairs={{1,0},{2,1},{3,2},{4,3},{5,4},{6,5},{7,6},{0,7},{9,8},{10,9},{11,1... | collective-permute-start | bytes 98312 | tf_op jit(solution)/shard_map/ppermute | solution.py:20
  63.4 5.3 %collective-permute-start.2 = (bf16[32,4,1,128]{3,0,2,1:T(8,128)(2,1)S(1)}, bf16[32,4,1,128]{3,0,2,1:T(8,128)(2,1)S(1)}, u32[]{:S(2)}, u32[]{:S(2)}) collective-permute-start(bf16[32,4,1,128]{3,0,2,1:T(8,128)(2,1)S(1)} %get-tuple-element.140), channel_id=1, source_target_pairs={{0,1},{1,2},{2,3},{3,4},{4,5},{5,6},{6,7},{7,0},{8,9},{9,10},{10,1... | collective-permute-start | bytes 98312 | tf_op jit(solution)/shard_map/ppermute | solution.py:18
  65.7 110.3 %collective-permute-start.15 = (bf16[32,4,1,128]{3,0,2,1:T(8,128)(2,1)}, bf16[32,4,1,128]{3,0,2,1:T(8,128)(2,1)S(1)}, u32[]{:S(2)}, u32[]{:S(2)}) collective-permute-start(bf16[32,4,1,128]{3,0,2,1:T(8,128)(2,1)} %get-tuple-element.133), channel_id=1, source_target_pairs={{1,0},{2,1},{3,2},{4,3},{5,4},{6,5},{7,6},{0,7},{9,8},{10,9},{11,1... | collective-permute-start | bytes 98312 | tf_op jit(solution)/shard_map/ppermute | solution.py:20
  68.6 107.3 %collective-permute-start.14 = (bf16[32,4,1,128]{3,0,2,1:T(8,128)(2,1)S(1)}, bf16[32,4,1,128]{3,0,2,1:T(8,128)(2,1)S(1)}, u32[]{:S(2)}, u32[]{:S(2)}) collective-permute-start(bf16[32,4,1,128]{3,0,2,1:T(8,128)(2,1)S(1)} %get-tuple-element.132), channel_id=1, source_target_pairs={{0,1},{1,2},{2,3},{3,4},{4,5},{5,6},{6,7},{7,0},{8,9},{9,10},{10,1... | collective-permute-start | bytes 98312 | tf_op jit(solution)/shard_map/ppermute | solution.py:18
  78.7 1.2 copy-start.1
  82.4 1.1 copy-start
  83.8 115.5 %collective-permute-start.5 = (bf16[32,1,32,128]{3,0,2,1:T(8,128)(2,1)}, bf16[32,1,32,128]{3,0,2,1:T(8,128)(2,1)S(1)}, u32[]{:S(2)}, u32[]{:S(2)}) collective-permute-start(bf16[32,1,32,128]{3,0,2,1:T(8,128)(2,1)} %get-tuple-element.149), channel_id=1, source_target_pairs={{8,0},{16,8},{24,16},{32,24},{40,32},{48,40},{56,48},{64,56},{72,6... | collective-permute-start | bytes 786440 | tf_op jit(solution)/shard_map/ppermute | solution.py:20
  92.6 106.7 %collective-permute-start.4 = (bf16[32,1,32,128]{3,0,2,1:T(8,128)(2,1)}, bf16[32,1,32,128]{3,0,2,1:T(8,128)(2,1)S(1)}, u32[]{:S(2)}, u32[]{:S(2)}) collective-permute-start(bf16[32,1,32,128]{3,0,2,1:T(8,128)(2,1)} %get-tuple-element.148), channel_id=1, source_target_pairs={{0,8},{8,16},{16,24},{24,32},{32,40},{40,48},{48,56},{56,64},{64,7... | collective-permute-start | bytes 786440 | tf_op jit(solution)/shard_map/ppermute | solution.py:18
  199.3 247.3 %collective-permute-start.7 = (bf16[32,4,1,128]{3,0,2,1:T(8,128)(2,1)S(1)}, bf16[32,4,1,128]{3,0,2,1:T(8,128)(2,1)S(1)}, u32[]{:S(2)}, u32[]{:S(2)}) collective-permute-start(bf16[32,4,1,128]{3,0,2,1:T(8,128)(2,1)S(1)} %get-tuple-element.137), channel_id=1, source_target_pairs={{1,0},{2,1},{3,2},{4,3},{5,4},{6,5},{7,6},{0,7},{9,8},{10,9},{11,1... | collective-permute-start | bytes 98312 | tf_op jit(solution)/shard_map/ppermute | solution.py:20
  200.8 245.9 %collective-permute-start.6 = (bf16[32,4,1,128]{3,0,2,1:T(8,128)(2,1)S(1)}, bf16[32,4,1,128]{3,0,2,1:T(8,128)(2,1)S(1)}, u32[]{:S(2)}, u32[]{:S(2)}) collective-permute-start(bf16[32,4,1,128]{3,0,2,1:T(8,128)(2,1)S(1)} %get-tuple-element.136), channel_id=1, source_target_pairs={{0,1},{1,2},{2,3},{3,4},{4,5},{5,6},{6,7},{7,0},{8,9},{9,10},{10,1... | collective-permute-start | bytes 98312 | tf_op jit(solution)/shard_map/ppermute | solution.py:18
Sparse Core Ops, SparseCore 0:
  199.4 245.6 all-reduce.1
where the time goes:
time: 475 us; the launch traced here: 466 us
  waiting for transfers between devices  248 us (52%)
  blocking collectives  82.1 us (17%)
  local copies, waits for them, and re-layouts  34.8 us (7%)
  starting transfers between devices  31.9 us (7%)
  other arithmetic  31.8 us (7%)
  matrix products  22.3 us (5%)
  between operations  15.2 us (3%)
    psum x1, waiting for transfers between devices, on_device(): summed = lax.psum((first_terms, second_terms), ('gx', 'gy'))  244 us
    psum x1, blocking collectives, on_device(): summed = lax.psum((first_terms, second_terms), ('gx', 'gy'))  82.1 us
    ppermute x8, starting transfers between devices, extended(): lax.ppermute(head, axis, [((i + 1) % count, i) for i in range(count)])  26.9 us
    another operation x30, local copies, waits for them, and re-layouts, tap_block(): jnp.stack([rolled[tap_z][:, shift_x:shift_x + size_x, tap_y:tap_y + size_...  21.6 us
    unnamed x35, other arithmetic  16.4 us
    dot_general x6, matrix products, weight_terms(): jnp.einsum('oxyz,tcxyz->otc', grad_vals, tap_block(rolled, tap_x, size_x,...  11.4 us
    dot_general x9, matrix products, correlate(): jnp.einsum('tcxyz,otc->oxyz', stacked, weights[:, 9 * tap_x:9 * tap_x + 9...  10.9 us
  transfers between devices with their start and end apart: 17, of which 4 were waited for; matrix products, arithmetic and copies ran while one was open for 16% of the time, Pallas kernels for 0%

commit v1 on v0

v1 whole, which is shorter than its diff:
```python
import functools
import math

import jax
import jax.numpy as jnp
from jax import lax
from jax.experimental import pallas as pl
from jax.experimental.pallas import tpu as pltpu
from jax.sharding import PartitionSpec as P

MESH = pl.DeviceIdType.MESH
SLOPE = 0.01
F32 = jnp.float32
BF16 = jnp.bfloat16
NT = (((1,), (1,)), ((), ()))


def factor(mask):
    return jnp.where(mask == 1, 1.0, SLOPE).astype(F32)


def shift(values, amount):
    return pltpu.roll(values, amount % 128, 1) if amount else values


def pair_of_rows(ref, planes, row):
    sides = []
    for side in range(2):
        blocks = []
        for plane in planes:
            block = ref[plane, pl.ds(row + side, 3)]
            blocks.append(block.reshape(block.shape[0] * block.shape[1], block.shape[2]))
        sides.append(jnp.concatenate(blocks, axis=0))
    return jnp.concatenate(sides, axis=1)


def kernel(
    nx, ny, scale,
    cot_in, mask1_in, mask2_in, field_in, a1, a2, a3, bias,
    grad_out, weights_out,
    cot_raw, mask1, mask2, field_raw, pad_cot, factors, pad_field, hid3, grad, acc2, acc1,
    part, part_x, got_x, got_y, got_c, mine, got_gx, row_sum, got_gy,
    local_sem, f_send, f_recv, p_send, p_recv, o_send, o_recv, s1_send, s1_recv, s2_send, s2_recv,
):
    gx = lax.axis_index("gx")
    gy = lax.axis_index("gy")

    loads = [
        pltpu.make_async_copy(cot_in, cot_raw, local_sem.at[0]),
        pltpu.make_async_copy(mask2_in, mask2, local_sem.at[1]),
        pltpu.make_async_copy(field_in, field_raw.at[:, 1:3, 16:48], local_sem.at[2]),
        pltpu.make_async_copy(mask1_in, mask1, local_sem.at[3]),
    ]
    for load in loads:
        load.start()

    left, right = lax.rem(gx + nx - 1, nx), lax.rem(gx + 1, nx)
    down, up = lax.rem(gy + ny - 1, ny), lax.rem(gy + 1, ny)

    barrier = pltpu.get_barrier_semaphore()

    def greet_x(k, _):
        pl.semaphore_signal(barrier, inc=1, device_id=(lax.rem(gx + k, nx), gy), device_id_type=MESH)
        return 0

    def greet_y(k, _):
        pl.semaphore_signal(barrier, inc=1, device_id=(gx, lax.rem(gy + k, ny)), device_id_type=MESH)
        return 0

    lax.fori_loop(1, nx, greet_x, 0)
    lax.fori_loop(1, ny, greet_y, 0)
    for corner in ((left, down), (left, up), (right, down), (right, up)):
        pl.semaphore_signal(barrier, inc=1, device_id=corner, device_id_type=MESH)

    loads[0].wait()
    loads[1].wait()
    for x in range(2):
        for half in range(2):
            rows = slice(16 * half, 16 * half + 16)
            values = cot_raw[:, x, rows, :].astype(F32) * factor(mask2[:, x, rows, :])
            pad_cot[x + 1, 1 + 16 * half : 17 + 16 * half] = jnp.swapaxes(values, 0, 1).astype(BF16)

    pl.semaphore_wait(barrier, (nx - 1) + (ny - 1) + 4)

    def remote(src, dst, send, recv, where):
        return pltpu.make_async_remote_copy(
            src_ref=src, dst_ref=dst, send_sem=send, recv_sem=recv, device_id=where, device_id_type=MESH
        )

    places = [(left, gy), (right, gy), (gx, down), (gx, up), (left, down), (left, up), (right, down), (right, up)]
    low, high = slice(0, 16), slice(16, 32)
    inner = slice(16, 48)
    field_moves = [
        (field_in.at[:, 0:1], field_raw.at[:, 3:4, inner]),
        (field_in.at[:, 1:2], field_raw.at[:, 0:1, inner]),
        (field_in.at[:, :, low], field_raw.at[:, 1:3, 48:64]),
        (field_in.at[:, :, high], field_raw.at[:, 1:3, 0:16]),
        (field_in.at[:, 0:1, low], field_raw.at[:, 3:4, 48:64]),
        (field_in.at[:, 0:1, high], field_raw.at[:, 3:4, 0:16]),
        (field_in.at[:, 1:2, low], field_raw.at[:, 0:1, 48:64]),
        (field_in.at[:, 1:2, high], field_raw.at[:, 0:1, 0:16]),
    ]
    cot_moves = [
        (pad_cot.at[1:2, 1:33], pad_cot.at[3:4, 1:33]),
        (pad_cot.at[2:3, 1:33], pad_cot.at[0:1, 1:33]),
        (pad_cot.at[1:3, 1:2], pad_cot.at[1:3, 33:34]),
        (pad_cot.at[1:3, 32:33], pad_cot.at[1:3, 0:1]),
        (pad_cot.at[1:2, 1:2], pad_cot.at[3:4, 33:34]),
        (pad_cot.at[1:2, 32:33], pad_cot.at[3:4, 0:1]),
        (pad_cot.at[2:3, 1:2], pad_cot.at[0:1, 33:34]),
        (pad_cot.at[2:3, 32:33], pad_cot.at[0:1, 0:1]),
    ]
    field_copies = [
        remote(src, dst, f_send.at[i], f_recv.at[i], places[i]) for i, (src, dst) in enumerate(field_moves)
    ]
    cot_copies = [
        remote(src, dst, p_send.at[i], p_recv.at[i], places[i]) for i, (src, dst) in enumerate(cot_moves)
    ]
    for copy in field_copies:
        copy.start()
    for copy in cot_copies:
        copy.start()

    loads[3].wait()
    for x in range(2):
        for half in range(2):
            rows = slice(16 * half, 16 * half + 16)
            factors[x, rows] = jnp.swapaxes(factor(mask1[:, x, rows, :]), 0, 1)

    loads[2].wait()
    for copy in field_copies:
        copy.wait_recv()

    def spread(plane, _):
        for block in range(4):
            rows = []
            for channel in range(3):
                row = field_raw[channel, plane, 16 * block : 16 * block + 16, :].astype(F32)
                rows.extend([shift(row, 1), row, shift(row, -1)])
            rows.extend([jnp.zeros((16, 128), F32)] * 7)
            pad_field[plane, 16 * block : 16 * block + 16] = jnp.swapaxes(jnp.stack(rows, axis=0), 0, 1).astype(BF16)
        return 0

    lax.fori_loop(0, 4, spread, 0)

    def forward(i, _):
        rhs = pair_of_rows(pad_field, range(4), 2 * i + 15)
        pre = jnp.dot(a1[...], rhs, preferred_element_type=F32) + bias[...]
        act = jnp.where(pre >= 0, pre, SLOPE * pre).astype(BF16).astype(F32)
        for x in range(2):
            for tap in range(3):
                for side in range(2):
                    block = shift(act[32 * x : 32 * x + 32, 128 * side : 128 * side + 128], 1 - tap)
                    hid3[i, x, 32 * tap : 32 * tap + 32, 128 * side : 128 * side + 128] = block.astype(BF16)
        return 0

    lax.fori_loop(0, 16, forward, 0)

    for x in range(2):
        for rows in (slice(0, 2), slice(34, 36)):
            grad[x, rows] = jnp.zeros((2, 32, 128), BF16)
    acc2[...] = jnp.zeros_like(acc2)
    acc1[...] = jnp.zeros_like(acc1)
    mine[...] = jnp.zeros_like(mine)

    for copy in cot_copies:
        copy.wait_recv()

    def second(i, _):
        rows = pair_of_rows(pad_cot, range(4), 2 * i)
        total = lax.dot_general(rows[0:288], hid3[i, 0], NT, preferred_element_type=F32)
        total += lax.dot_general(rows[96:384], hid3[i, 1], NT, preferred_element_type=F32)
        acc2[...] += total
        return 0

    lax.fori_loop(0, 16, second, 0)
    for tap in range(9):
        mine[:, tap, 0:96] = acc2[32 * tap : 32 * tap + 32, :]

    def backward(i, _):
        rows = pair_of_rows(pad_cot, range(4), 2 * i)
        out = jnp.dot(a2[...], rows, preferred_element_type=F32)
        for x in range(2):
            for side in range(2):
                total = None
                for tap in range(3):
                    start = 96 * x + 32 * tap
                    term = shift(out[start : start + 32, 128 * side : 128 * side + 128], tap - 1)
                    total = term if total is None else total + term
                grad[x, 2 * i + side + 2] = (total * factors[x, 2 * i + side]).astype(BF16)
        return 0

    lax.fori_loop(0, 16, backward, 0)

    def first(i, _):
        rows = pair_of_rows(pad_field, range(4), 2 * i + 15)
        total = None
        for x in range(2):
            cells = jnp.concatenate([grad[x, 2 * i + 2], grad[x, 2 * i + 3]], axis=1)
            term = lax.dot_general(cells, rows[48 * x : 48 * x + 144], NT, preferred_element_type=F32)
            total = term if total is None else total + term
        acc1[...] += total
        return 0

    lax.fori_loop(0, 16, first, 0)
    mine[:, 9, :] = acc1[:, 0:128]
    mine[:, 10, 0:16] = acc1[:, 128:144]

    def send_row(k, _):
        to = lax.rem(gx + k, nx)
        remote(mine.at[to], got_gx.at[k], s1_send.at[k], s1_recv.at[k], (to, gy)).start()
        return 0

    lax.fori_loop(1, nx, send_row, 0)

    def scatter(i, _):
        rows = pair_of_rows(grad, range(2), 2 * i)
        out = jnp.dot(a3[...], rows, preferred_element_type=F32)
        for plane in range(4):
            for side in range(2):
                total = None
                for tap in range(3):
                    start = 24 * plane + 8 * tap
                    term = shift(out[start : start + 8, 128 * side : 128 * side + 128], tap - 1)
                    total = term if total is None else total + term
                part[plane, 2 * i + side] = total
        return 0

    lax.fori_loop(0, 17, scatter, 0)
    part_x[0] = jnp.swapaxes(part[0, 1:33], 0, 1)[0:3]
    part_x[1] = jnp.swapaxes(part[3, 1:33], 0, 1)[0:3]

    part_moves = [
        (part_x.at[0], got_x.at[1]),
        (part_x.at[1], got_x.at[0]),
        (part.at[1:3, 0], got_y.at[1]),
        (part.at[1:3, 33], got_y.at[0]),
        (part.at[0, 0], got_c.at[3]),
        (part.at[0, 33], got_c.at[2]),
        (part.at[3, 0], got_c.at[1]),
        (part.at[3, 33], got_c.at[0]),
    ]
    part_copies = [
        remote(src, dst, o_send.at[i], o_recv.at[i], places[i]) for i, (src, dst) in enumerate(part_moves)
    ]
    for copy in part_copies:
        copy.start()

    def take_row(k, total):
        to = lax.rem(gx + k, nx)
        remote(mine.at[to], got_gx.at[k], s1_send.at[k], s1_recv.at[k], (to, gy)).wait_recv()
        return total + got_gx[k]

    row_sum[...] = lax.fori_loop(1, nx, take_row, mine[gx])

    def send_sum(k, _):
        to = lax.rem(gy + k, ny)
        remote(row_sum, got_gy.at[k], s2_send.at[k], s2_recv.at[k], (gx, to)).start()
        return 0

    lax.fori_loop(1, ny, send_sum, 0)

    for copy in part_copies:
        copy.wait_recv()
    for x in range(2):
        part[x + 1, 1] += got_y[0, x]
        part[x + 1, 32] += got_y[1, x]
        part[x + 1, 1] += got_c[2 * x]
        part[x + 1, 32] += got_c[2 * x + 1]
    for x in range(2):
        grad_out[:, x] = jnp.swapaxes(part[x + 1, 1:33], 0, 1)[0:3] + got_x[x]

    def take_sum(k, total):
        to = lax.rem(gy + k, ny)
        remote(row_sum, got_gy.at[k], s2_send.at[k], s2_recv.at[k], (gx, to)).wait_recv()
        return total + got_gy[k]

    weights_out[...] = lax.fori_loop(1, ny, take_sum, row_sum[...]) * scale

    for copy in field_copies + cot_copies + part_copies:
        copy.wait_send()

    def sent_row(k, _):
        to = lax.rem(gx + k, nx)
        remote(mine.at[to], got_gx.at[k], s1_send.at[k], s1_recv.at[k], (to, gy)).wait_send()
        return 0

    def sent_sum(k, _):
        to = lax.rem(gy + k, ny)
        remote(row_sum, got_gy.at[k], s2_send.at[k], s2_recv.at[k], (gx, to)).wait_send()
        return 0

    lax.fori_loop(1, nx, sent_row, 0)
    lax.fori_loop(1, ny, sent_sum, 0)


def weight_forms(conv_first, conv_second):
    first = conv_first.reshape(32, 3, 3, 3, 3)
    second = conv_second.reshape(32, 3, 3, 3, 32)
    w1 = jnp.pad(first.transpose(0, 1, 2, 4, 3).reshape(32, 9, 9), ((0, 0), (0, 0), (0, 7))).reshape(32, 144)
    a1 = jnp.concatenate([jnp.pad(w1, ((0, 0), (0, 48))), jnp.pad(w1, ((0, 0), (48, 0)))], axis=0)
    w2 = second[:, ::-1, ::-1].transpose(3, 4, 1, 2, 0).reshape(96, 288)
    a2 = jnp.concatenate([jnp.pad(w2, ((0, 0), (0, 96))), jnp.pad(w2, ((0, 0), (96, 0)))], axis=0)
    w3 = jnp.pad(first[:, :, ::-1].transpose(1, 3, 4, 2, 0), ((0, 0), (0, 0), (0, 5), (0, 0), (0, 0))).reshape(3, 24, 96)
    none = jnp.zeros((24, 96), BF16)
    a3 = jnp.concatenate(
        [
            jnp.concatenate([w3[p - g] if 0 <= p - g < 3 else none for g in range(2)], axis=1)
            for p in range(4)
        ],
        axis=0,
    )
    return a1, a2, a3


def on_device(nx, ny, field_in, conv_first, bias_first, conv_second, cotangent, mask_first, mask_second):
    a1, a2, a3 = weight_forms(conv_first, conv_second)
    bias = jnp.broadcast_to(jnp.concatenate([bias_first, bias_first])[:, None], (64, 256))
    scale = 1.0 / math.sqrt(2 * nx * 32 * ny * 128)
    anywhere = pl.BlockSpec(memory_space=pl.ANY)
    vmem = pl.BlockSpec(memory_space=pltpu.VMEM)
    dma = pltpu.SemaphoreType.DMA
    input_grad, weights = pl.pallas_call(
        functools.partial(kernel, nx, ny, scale),
        out_shape=(
            jax.ShapeDtypeStruct((3, 2, 32, 128), F32),
            jax.ShapeDtypeStruct((11, 128), F32),
        ),
        in_specs=[anywhere] * 4 + [vmem] * 4,
        out_specs=(vmem, vmem),
        scratch_shapes=[
            pltpu.VMEM((32, 2, 32, 128), BF16),
            pltpu.VMEM((32, 2, 32, 128), jnp.int32),
            pltpu.VMEM((32, 2, 32, 128), jnp.int32),
            pltpu.VMEM((3, 4, 64, 128), BF16),
            pltpu.VMEM((4, 34, 32, 128), BF16),
            pltpu.VMEM((2, 32, 32, 128), F32),
            pltpu.VMEM((4, 64, 16, 128), BF16),
            pltpu.VMEM((16, 2, 96, 256), BF16),
            pltpu.VMEM((2, 36, 32, 128), BF16),
            pltpu.VMEM((288, 96), F32),
            pltpu.VMEM((32, 144), F32),
            pltpu.VMEM((4, 34, 8, 128), F32),
            pltpu.VMEM((2, 3, 32, 128), F32),
            pltpu.VMEM((2, 3, 32, 128), F32),
            pltpu.VMEM((2, 2, 8, 128), F32),
            pltpu.VMEM((4, 8, 128), F32),
            pltpu.VMEM((32, 11, 128), F32),
            pltpu.VMEM((nx, 11, 128), F32),
            pltpu.VMEM((11, 128), F32),
            pltpu.VMEM((ny, 11, 128), F32),
            dma((4,)),
            dma((8,)),
            dma((8,)),
            dma((8,)),
            dma((8,)),
            dma((8,)),
            dma((8,)),
            dma((nx,)),
            dma((nx,)),
            dma((ny,)),
            dma((ny,)),
        ],
        compiler_params=pltpu.CompilerParams(
            collective_id=0, has_side_effects=True, vmem_limit_bytes=40 * 1024 * 1024
        ),
    )(cotangent, mask_first, mask_second, field_in, a1, a2, a3, bias)
    grad_second = weights[0:9, 0:96].reshape(3, 3, 3, 32)[::-1, ::-1].reshape(1, 27, 32)
    tail = jnp.concatenate([weights[9], weights[10, 0:16]]).reshape(9, 16)[:, 0:9]
    grad_first = tail.reshape(9, 3, 3).transpose(0, 2, 1).reshape(1, 27, 3)
    return input_grad, grad_first, grad_second


def solution(mesh):
    cells = P(None, "gx", "gy", None)
    return jax.shard_map(
        functools.partial(on_device, mesh.shape["gx"], mesh.shape["gy"]),
        mesh=mesh,
        in_specs=(cells, P(), P(), P(), cells, cells, cells),
        out_specs=(cells, P("gx", None, None), P("gx", None, None)),
        check_vma=False,
    )
```

time: 475 us -> 54.3 us (0.11); the launches traced: 466 us -> 54.2 us
  waiting for transfers between devices: 248 us -> 0 us
  blocking collectives: 82.1 us -> 0 us
  Pallas kernels: 0 us -> 46.3 us
  starting transfers between devices: 31.9 us -> 0 us
  other arithmetic: 31.8 us -> 0.36 us
  local copies, waits for them, and re-layouts: 34.8 us -> 6.71 us
  matrix products: 22.3 us -> 0 us
  between operations: 15.2 us -> 0.8 us
    psum x1 -> x0, waiting for transfers between devices: 244 us -> none  [on_device(): summed = lax.psum((first_terms, second_terms), ('gx', 'gy'))]
    psum x1 -> x0, blocking collectives: 82.1 us -> none  [on_device(): summed = lax.psum((first_terms, second_terms), ('gx', 'gy'))]
    pallas_call x0 -> x1, Pallas kernels: none -> 46.3 us  [on_device(): pl.pallas_call(functools.partial(kernel, nx, ny, scale), out_shape=(jax.S...]
    ppermute x16 -> x0, starting transfers between devices: 31.9 us -> none  [the longest x8 26.9 us: extended(): lax.ppermute(head, axis, [((i + 1) % count, i) for i in range(count)])]
    dot_general x15 -> x0, matrix products: 22.3 us -> none  [the longest x6 11.4 us: weight_terms(): jnp.einsum('oxyz,tcxyz->otc', grad_vals, tap_block(rolled, tap_x, size_x,...]
    another operation x30 -> x0, local copies, waits for them, and re-layouts: 21.6 us -> none  [tap_block(): jnp.stack([rolled[tap_z][:, shift_x:shift_x + size_x, tap_y:tap_y + size_...]
    unnamed x35 -> x0, other arithmetic: 16.4 us -> none
    slice x13 -> x5, local copies, waits for them, and re-layouts: 6.55 us -> 0.16 us  [the longest x1 0.1 us: on_device(): jnp.concatenate([weights[9], weights[10, 0:16]]).reshape(9, 16)[:, 0:9]]
  transfers between devices with their start and end apart: 17 -> 0, of which waited for: 4 -> 0; matrix products, arithmetic and copies ran while one was open for 16% -> 0% of each run, Pallas kernels for 0% -> 0%
where the time goes in v1:
time: 54.3 us; the launch traced here: 54.2 us
  Pallas kernels  46.3 us (85%)
  local copies, waits for them, and re-layouts  6.71 us (12%)
  between operations  0.8 us (1%)
    pallas_call x1, Pallas kernels, on_device(): pl.pallas_call(functools.partial(kernel, nx, ny, scale), out_shape=(jax.S...  46.3 us
    unnamed x12, local copies, waits for them, and re-layouts  2.34 us
    reshape x1, local copies, waits for them, and re-layouts, weight_forms(): second = conv_second.reshape(32, 3, 3, 3, 32)  1.27 us

profile of v1, /device:TPU:1, one launch (start us, length us, event | category | flops | bytes accessed | tf_op | source)
XLA Modules:
  0.0 54.2 jit_solution(13972801394578412560)
XLA Ops:
  0.6 0.0 copy-start.2
  0.6 0.9 %copy.15 = bf16[32,27,3]{0,1,2:T(8,128)(2,1)S(1)} copy(bf16[32,27,3]{1,0,2:T(8,128)(2,1)} %param.8) | data formatting | bytes 10368 | tf_op args[1]
  1.6 0.1 copy.17
  1.7 0.0 copy-start.4
  1.7 0.1 fusion.10.a1
  1.8 0.0 copy-start
  1.8 0.0 copy-start.1
  1.8 1.3 %copy.19 = bf16[32,3,3,3,32]{0,2,1,4,3:T(4,128)(2,1)S(1)} copy(bf16[32,3,3,3,32]{4,0,3,2,1:T(8,128)(2,1)} %bitcast.24) | data formatting | bytes 110592 | tf_op jit(solution)/shard_map/reshape | solution.py:299
  3.1 0.7 %rev.9 = bf16[32,3,3,3,32]{0,2,1,4,3:T(4,128)(2,1)S(1)} reverse(bf16[32,3,3,3,32]{0,2,1,4,3:T(4,128)(2,1)S(1)} %copy.19), dimensions={1,2} | reverse | bytes 110592 | tf_op jit(solution)/shard_map/rev | solution.py:302
  3.8 0.2 reshape.48
  4.0 0.1 fusion.2.a2
  4.1 0.1 squeeze.20
  4.3 0.1 squeeze.18
  4.4 0.1 squeeze.19
  4.4 0.1 fusion.7.a3
  4.5 0.0 copy-done.4
  4.5 0.1 pad_maximum_fusion.1
  4.6 0.1 broadcast_in_dim.2.bias
  4.7 0.0 copy-done.2
  4.7 0.0 copy-done
  4.7 0.0 copy-done.1
  4.7 0.0 copy-start.3
  4.7 0.8 %copy-done.3 = bf16[3,2,32,128]{3,2,1,0:T(8,128)(2,1)S(1)} copy-done((bf16[3,2,32,128]{3,2,1,0:T(8,128)(2,1)S(1)}, bf16[3,2,32,128]{3,2,1,0:T(8,128)(2,1)}, u32[]{:S(2)}) %copy-start.3) | copy-done | bytes 49176
  5.5 46.3 %shard_map.94 = (f32[3,2,32,128]{3,2,1,0:T(8,128)S(1)}, f32[11,128]{1,0:T(8,128)S(1)}) custom-call(bf16[32,2,32,128]{3,2,1,0:T(8,128)(2,1)S(1)} %copy-done.2, s32[32,2,32,128]{3,2,1,0:T(8,128)S(1)} %copy-done, s32[32,2,32,128]{3,2,1,0:T(8,128)S(1)} %copy-done.1, bf16[3,2,32,128]{3,2,1,0:T(8,128)(2,1)S(1)} %copy-done.3, bf16[64,192]{1,0:T(8,128)(2,1)S(1)} %fusion.10.a1, ...), custom_call_target="tpu_custom_call" | custom-call | tf_op jit(solution)/shard_map/pallas_call | solution.py:323
  51.9 0.1 reshape.49
  51.9 0.1 copy.23
  52.1 0.1 copy.24
  52.2 0.7 %reshape.54 = f32[1,27,3]{1,0,2:T(1,128)} reshape(f32[9,3,3]{1,0,2:T(8,128)S(1)} %copy.24) | data formatting | bytes 648 | tf_op jit(solution)/shard_map/reshape | solution.py:370
  52.8 0.1 reshape.52
  52.9 0.6 %reshape.53 = f32[1,27,32]{2,0,1:T(1,128)} reshape(f32[3,3,3,32]{3,2,1,0:T(4,128)S(1)} %rev.11) | data formatting | bytes 6912 | tf_op jit(solution)/shard_map/reshape | solution.py:368
  53.5 0.6 %copy.27 = f32[3,2,32,128]{3,2,1,0:T(8,128)} copy(f32[3,2,32,128]{3,2,1,0:T(8,128)S(1)} %get-tuple-element.19) | data formatting | bytes 196608
  (14 shorter events, 0.2 us)
Async XLA Ops:
  0.6 4.1 %copy-start.2 = (bf16[32,2,32,128]{3,2,1,0:T(8,128)(2,1)S(1)}, bf16[32,2,32,128]{3,2,1,0:T(8,128)(2,1)}, u32[]{:S(2)}) copy-start(bf16[32,2,32,128]{3,2,1,0:T(8,128)(2,1)} %cot_in.1) | copy-start | bytes 1572868
  1.7 2.8 %copy-start.4 = (f32[32]{0:T(128)S(1)}, f32[32]{0:T(128)}, u32[]{:S(2)}) copy-start(f32[32]{0:T(128)} %param.9) | copy-start | bytes 388
  1.8 2.9 %copy-start = (s32[32,2,32,128]{3,2,1,0:T(8,128)S(1)}, s32[32,2,32,128]{3,2,1,0:T(8,128)}, u32[]{:S(2)}) copy-start(s32[32,2,32,128]{3,2,1,0:T(8,128)} %mask1_in.1) | copy-start | bytes 3145732
  1.8 2.9 %copy-start.1 = (s32[32,2,32,128]{3,2,1,0:T(8,128)S(1)}, s32[32,2,32,128]{3,2,1,0:T(8,128)}, u32[]{:S(2)}) copy-start(s32[32,2,32,128]{3,2,1,0:T(8,128)} %mask2_in.1) | copy-start | bytes 3145732
  4.7 0.8 %copy-start.3 = (bf16[3,2,32,128]{3,2,1,0:T(8,128)(2,1)S(1)}, bf16[3,2,32,128]{3,2,1,0:T(8,128)(2,1)}, u32[]{:S(2)}) copy-start(bf16[3,2,32,128]{3,2,1,0:T(8,128)(2,1)} %field_in.1) | copy-start | bytes 147460

commit v2 on v1

v2 whole, which is shorter than its diff:
```python
import functools
import math

import jax
import jax.numpy as jnp
from jax import lax
from jax.experimental import pallas as pl
from jax.experimental.pallas import tpu as pltpu
from jax.sharding import PartitionSpec as P

MESH = pl.DeviceIdType.MESH
SLOPE = 0.01
F32 = jnp.float32
BF16 = jnp.bfloat16
NT = (((1,), (1,)), ((), ()))


def factor(mask):
    return jnp.where(mask == 1, 1.0, SLOPE).astype(F32)


def shift(values, amount):
    return pltpu.roll(values, amount % 128, 1) if amount else values


def beside(ref, planes, row, count):
    sides = []
    for side in range(count):
        blocks = []
        for plane in planes:
            block = ref[plane, pl.ds(row + side, 3)]
            blocks.append(block.reshape(block.shape[0] * block.shape[1], block.shape[2]))
        sides.append(jnp.concatenate(blocks, axis=0) if len(blocks) > 1 else blocks[0])
    return jnp.concatenate(sides, axis=1)


def kernel(
    nx, ny, scale,
    cot_in, mask1_in, mask2_in, field_in, first_in, second_in, bias_in,
    grad_out, first_out, second_out,
    cot_raw, mask1, mask2, field_raw, first_raw, second_raw, bias_raw,
    pad_cot, factors, pad_field, hid3, grad, hidden_grad, acc2, acc1,
    form1, form2, form2_far, form3, turn2, turn3, bias,
    part, part_x, got_x, got_y, got_c, mine, got_gx, row_sum, got_gy,
    local_sem, f_send, f_recv, p_send, p_recv, o_send, o_recv, s1_send, s1_recv, s2_send, s2_recv,
):
    gx = lax.axis_index("gx")
    gy = lax.axis_index("gy")

    loads = [
        pltpu.make_async_copy(cot_in, cot_raw, local_sem.at[0]),
        pltpu.make_async_copy(mask2_in, mask2, local_sem.at[1]),
        pltpu.make_async_copy(field_in, field_raw.at[:, 1:3, 16:48], local_sem.at[2]),
        pltpu.make_async_copy(mask1_in, mask1, local_sem.at[3]),
        pltpu.make_async_copy(first_in, first_raw, local_sem.at[4]),
        pltpu.make_async_copy(second_in, second_raw, local_sem.at[5]),
        pltpu.make_async_copy(bias_in, bias_raw, local_sem.at[6]),
    ]
    for load in loads:
        load.start()

    left, right = lax.rem(gx + nx - 1, nx), lax.rem(gx + 1, nx)
    down, up = lax.rem(gy + ny - 1, ny), lax.rem(gy + 1, ny)

    barrier = pltpu.get_barrier_semaphore()

    def greet_x(k, _):
        pl.semaphore_signal(barrier, inc=1, device_id=(lax.rem(gx + k, nx), gy), device_id_type=MESH)
        return 0

    def greet_y(k, _):
        pl.semaphore_signal(barrier, inc=1, device_id=(gx, lax.rem(gy + k, ny)), device_id_type=MESH)
        return 0

    for corner in ((left, down), (left, up), (right, down), (right, up)):
        pl.semaphore_signal(barrier, inc=1, device_id=corner, device_id_type=MESH)
    lax.fori_loop(1, nx, greet_x, 0)
    lax.fori_loop(1, ny, greet_y, 0)

    loads[0].wait()
    loads[1].wait()
    for x in range(2):
        for half in range(2):
            rows = slice(16 * half, 16 * half + 16)
            values = cot_raw[:, x, rows, :].astype(F32) * factor(mask2[:, x, rows, :])
            pad_cot[x + 1, 1 + 16 * half : 17 + 16 * half] = jnp.swapaxes(values, 0, 1).astype(BF16)

    loads[2].wait()
    pl.semaphore_wait(barrier, (nx - 1) + (ny - 1) + 4)

    def remote(src, dst, send, recv, where):
        return pltpu.make_async_remote_copy(
            src_ref=src, dst_ref=dst, send_sem=send, recv_sem=recv, device_id=where, device_id_type=MESH
        )

    places = [(left, gy), (right, gy), (gx, down), (gx, up), (left, down), (left, up), (right, down), (right, up)]
    low, high = slice(16, 32), slice(32, 48)
    inner, before, after = slice(16, 48), slice(0, 16), slice(48, 64)
    field_moves = [
        (field_raw.at[:, 1:2, inner], field_raw.at[:, 3:4, inner]),
        (field_raw.at[:, 2:3, inner], field_raw.at[:, 0:1, inner]),
        (field_raw.at[:, 1:3, low], field_raw.at[:, 1:3, after]),
        (field_raw.at[:, 1:3, high], field_raw.at[:, 1:3, before]),
        (field_raw.at[:, 1:2, low], field_raw.at[:, 3:4, after]),
        (field_raw.at[:, 1:2, high], field_raw.at[:, 3:4, before]),
        (field_raw.at[:, 2:3, low], field_raw.at[:, 0:1, after]),
        (field_raw.at[:, 2:3, high], field_raw.at[:, 0:1, before]),
    ]
    cot_moves = [
        (pad_cot.at[1:2, 1:33], pad_cot.at[3:4, 1:33]),
        (pad_cot.at[2:3, 1:33], pad_cot.at[0:1, 1:33]),
        (pad_cot.at[1:3, 1:2], pad_cot.at[1:3, 33:34]),
        (pad_cot.at[1:3, 32:33], pad_cot.at[1:3, 0:1]),
        (pad_cot.at[1:2, 1:2], pad_cot.at[3:4, 33:34]),
        (pad_cot.at[1:2, 32:33], pad_cot.at[3:4, 0:1]),
        (pad_cot.at[2:3, 1:2], pad_cot.at[0:1, 33:34]),
        (pad_cot.at[2:3, 32:33], pad_cot.at[0:1, 0:1]),
    ]
    field_copies = [
        remote(src, dst, f_send.at[i], f_recv.at[i], places[i]) for i, (src, dst) in enumerate(field_moves)
    ]
    cot_copies = [
        remote(src, dst, p_send.at[i], p_recv.at[i], places[i]) for i, (src, dst) in enumerate(cot_moves)
    ]
    for copy in cot_copies[2:4] + field_copies + cot_copies[0:2] + cot_copies[4:8]:
        copy.start()

    loads[4].wait()
    loads[5].wait()
    loads[6].wait()
    form1[...] = jnp.zeros_like(form1)
    form2[...] = jnp.zeros_like(form2)
    form2_far[...] = jnp.zeros_like(form2_far)
    form3[...] = jnp.zeros_like(form3)
    turn2[...] = jnp.zeros_like(turn2)
    turn3[...] = jnp.zeros_like(turn3)
    taps1 = jnp.swapaxes(first_raw[...].astype(F32), 0, 1)
    taps2 = jnp.swapaxes(second_raw[...].astype(F32), 0, 1)
    for q in range(9):
        dx, dy = q // 3, q % 3
        back2 = 32 * (8 - q)
        back3 = 32 * (3 * dx + 2 - dy)
        for dz in range(3):
            form1[0:32, 16 * q + 3 * dz : 16 * q + 3 * dz + 3] = taps1[3 * q + dz]
            turn2[back2 : back2 + 32, 32 * dz : 32 * dz + 32] = taps2[3 * q + dz]
            turn3[back3 : back3 + 32, 8 * dz : 8 * dz + 3] = taps1[3 * q + dz]
    form1[32:64, 48:192] = form1[0:32, 0:144]
    whole2 = jnp.transpose(turn2[...])[0:96].astype(BF16)
    form2[0:96, 0:192] = whole2[:, 96:288]
    form2[96:192, 0:192] = whole2[:, 0:192]
    form2_far[0:96, 0:96] = whole2[:, 0:96]
    form2_far[96:192, 96:192] = whole2[:, 192:288]
    whole3 = jnp.transpose(turn3[...])[0:24]
    for plane in range(4):
        for x in range(2):
            if 0 <= plane - x < 3:
                form3[24 * plane : 24 * plane + 24, 96 * x : 96 * x + 96] = whole3[:, 96 * (plane - x) : 96 * (plane - x) + 96]
    across = jnp.transpose(jnp.broadcast_to(bias_raw[...], (8, 128)))[0:32, 0:1]
    bias[0:32] = jnp.broadcast_to(across, (32, 128))
    bias[32:64] = jnp.broadcast_to(across, (32, 128))

    loads[3].wait()
    for x in range(2):
        for half in range(2):
            rows = slice(16 * half, 16 * half + 16)
            factors[x, rows] = jnp.swapaxes(factor(mask1[:, x, rows, :]), 0, 1)

    for x in range(2):
        for rows in (slice(0, 2), slice(34, 36)):
            grad[x, rows] = jnp.zeros((2, 32, 128), BF16)
    mine[...] = jnp.zeros_like(mine)

    def turned(out, x, side):
        total = None
        for tap in range(3):
            start = 96 * x + 32 * tap
            term = shift(out[start : start + 32, 128 * side : 128 * side + 128], tap - 1)
            total = term if total is None else total + term
        return total

    cot_copies[2].wait_recv()
    cot_copies[3].wait_recv()

    def backward_near(i, _):
        out = jnp.dot(form2[...], beside(pad_cot, (1, 2), 8 * i, 8), preferred_element_type=F32)
        for x in range(2):
            for side in range(8):
                hidden_grad[x, 8 * i + side] = turned(out, x, side)
        return 0

    lax.fori_loop(0, 4, backward_near, 0)

    for copy in field_copies:
        copy.wait_recv()

    def spread(plane, _):
        for block in range(4):
            rows = []
            for dz in range(3):
                for channel in range(3):
                    row = field_raw[channel, plane, 16 * block : 16 * block + 16, :].astype(F32)
                    rows.append(shift(row, 1 - dz))
            rows.extend([jnp.zeros((16, 128), F32)] * 7)
            pad_field[plane, 16 * block : 16 * block + 16] = jnp.swapaxes(jnp.stack(rows, axis=0), 0, 1).astype(BF16)
        return 0

    lax.fori_loop(0, 4, spread, 0)
    form1_now = form1[...].astype(BF16)

    def forward(i, _):
        pre = jnp.dot(form1_now, beside(pad_field, range(4), 8 * i + 15, 8), preferred_element_type=F32)
        for x in range(2):
            for side in range(8):
                act = pre[32 * x : 32 * x + 32, 128 * side : 128 * side + 128] + bias[0:32]
                act = jnp.where(act >= 0, act, SLOPE * act).astype(BF16).astype(F32)
                for tap in range(3):
                    hid3[i, x, 32 * tap : 32 * tap + 32, 128 * side : 128 * side + 128] = shift(act, 1 - tap).astype(BF16)
        return 0

    lax.fori_loop(0, 4, forward, 0)

    acc2[...] = jnp.zeros_like(acc2)

    def second_near(i, _):
        rows = beside(pad_cot, (1, 2), 8 * i, 8)
        acc2[96:288] += lax.dot_general(rows, hid3[i, 0], NT, preferred_element_type=F32)
        acc2[0:192] += lax.dot_general(rows, hid3[i, 1], NT, preferred_element_type=F32)
        return 0

    lax.fori_loop(0, 4, second_near, 0)

    for copy in cot_copies[0:2] + cot_copies[4:8]:
        copy.wait_recv()

    def far(i, _):
        rows = beside(pad_cot, (0, 3), 8 * i, 8)
        acc2[0:96] += lax.dot_general(rows[0:96], hid3[i, 0], NT, preferred_element_type=F32)
        acc2[192:288] += lax.dot_general(rows[96:192], hid3[i, 1], NT, preferred_element_type=F32)
        out = jnp.dot(form2_far[...], rows, preferred_element_type=F32)
        for x in range(2):
            for side in range(8):
                total = hidden_grad[x, 8 * i + side] + turned(out, x, side)
                grad[x, 8 * i + side + 2] = (total * factors[x, 8 * i + side]).astype(BF16)
        return 0

    lax.fori_loop(0, 4, far, 0)

    acc1[...] = jnp.zeros_like(acc1)

    def first(i, _):
        rows = beside(pad_field, range(4), 8 * i + 15, 8)
        total = None
        for x in range(2):
            cells = jnp.concatenate([grad[x, 8 * i + 2 + side] for side in range(8)], axis=1)
            term = lax.dot_general(cells, rows[48 * x : 48 * x + 144], NT, preferred_element_type=F32)
            total = term if total is None else total + term
        acc1[...] += total
        return 0

    lax.fori_loop(0, 4, first, 0)
    for q in range(9):
        mine[:, q, 0:96] = acc2[32 * (8 - q) : 32 * (8 - q) + 32, :]
        mine[:, q, 96:105] = acc1[:, 16 * q : 16 * q + 9]

    def send_row(k, _):
        to = lax.rem(gx + k, nx)
        remote(mine.at[to], got_gx.at[k], s1_send.at[k], s1_recv.at[k], (to, gy)).start()
        return 0

    lax.fori_loop(1, nx, send_row, 0)

    form3_now = form3[...].astype(BF16)

    def scatter_rows(row, count):
        out = jnp.dot(form3_now, beside(grad, range(2), row, count), preferred_element_type=F32)
        for plane in range(4):
            for side in range(count):
                total = None
                for tap in range(3):
                    start = 24 * plane + 8 * tap
                    term = shift(out[start : start + 8, 128 * side : 128 * side + 128], tap - 1)
                    total = term if total is None else total + term
                part[plane, row + side] = total

    def scatter(i, _):
        scatter_rows(8 * i, 8)
        return 0

    lax.fori_loop(0, 4, scatter, 0)
    scatter_rows(32, 2)
    part_x[0] = jnp.swapaxes(part[0, 1:33], 0, 1)[0:3]
    part_x[1] = jnp.swapaxes(part[3, 1:33], 0, 1)[0:3]

    part_moves = [
        (part_x.at[0], got_x.at[1]),
        (part_x.at[1], got_x.at[0]),
        (part.at[1:3, 0], got_y.at[1]),
        (part.at[1:3, 33], got_y.at[0]),
        (part.at[0, 0], got_c.at[3]),
        (part.at[0, 33], got_c.at[2]),
        (part.at[3, 0], got_c.at[1]),
        (part.at[3, 33], got_c.at[0]),
    ]
    part_copies = [
        remote(src, dst, o_send.at[i], o_recv.at[i], places[i]) for i, (src, dst) in enumerate(part_moves)
    ]
    for copy in part_copies:
        copy.start()

    def take_row(k, total):
        to = lax.rem(gx + k, nx)
        remote(mine.at[to], got_gx.at[k], s1_send.at[k], s1_recv.at[k], (to, gy)).wait_recv()
        return total + got_gx[k]

    row_sum[...] = lax.fori_loop(1, nx, take_row, mine[gx])

    def send_sum(k, _):
        to = lax.rem(gy + k, ny)
        remote(row_sum, got_gy.at[k], s2_send.at[k], s2_recv.at[k], (gx, to)).start()
        return 0

    lax.fori_loop(1, ny, send_sum, 0)

    for copy in part_copies:
        copy.wait_recv()
    for x in range(2):
        part[x + 1, 1] += got_y[0, x]
        part[x + 1, 32] += got_y[1, x]
        part[x + 1, 1] += got_c[2 * x]
        part[x + 1, 32] += got_c[2 * x + 1]
    for x in range(2):
        grad_out[:, x] = jnp.swapaxes(part[x + 1, 1:33], 0, 1)[0:3] + got_x[x]

    def sent_row(k, _):
        to = lax.rem(gx + k, nx)
        remote(mine.at[to], got_gx.at[k], s1_send.at[k], s1_recv.at[k], (to, gy)).wait_send()
        return 0

    for copy in field_copies + cot_copies + part_copies:
        copy.wait_send()
    lax.fori_loop(1, nx, sent_row, 0)

    def take_sum(k, total):
        to = lax.rem(gy + k, ny)
        remote(row_sum, got_gy.at[k], s2_send.at[k], s2_recv.at[k], (gx, to)).wait_recv()
        return total + got_gy[k]

    total = lax.fori_loop(1, ny, take_sum, row_sum[...]) * scale
    for q in range(9):
        for dz in range(3):
            row = slice(3 * q + dz, 3 * q + dz + 1)
            second_out[0, row] = total[q : q + 1, 32 * dz : 32 * dz + 32]
            first_out[0, row] = total[q : q + 1, 96 + 3 * dz : 96 + 3 * dz + 3]

    def sent_sum(k, _):
        to = lax.rem(gy + k, ny)
        remote(row_sum, got_gy.at[k], s2_send.at[k], s2_recv.at[k], (gx, to)).wait_send()
        return 0

    lax.fori_loop(1, ny, sent_sum, 0)


def on_device(nx, ny, field_in, conv_first, bias_first, conv_second, cotangent, mask_first, mask_second):
    scale = 1.0 / math.sqrt(2 * nx * 32 * ny * 128)
    bias_row = jnp.pad(bias_first.reshape(1, 32), ((0, 0), (0, 96)))
    anywhere = pl.BlockSpec(memory_space=pl.ANY)
    vmem = pl.BlockSpec(memory_space=pltpu.VMEM)
    dma = pltpu.SemaphoreType.DMA
    input_grad, grad_first, grad_second = pl.pallas_call(
        functools.partial(kernel, nx, ny, scale),
        out_shape=(
            jax.ShapeDtypeStruct((3, 2, 32, 128), F32),
            jax.ShapeDtypeStruct((1, 27, 3), F32),
            jax.ShapeDtypeStruct((1, 27, 32), F32),
        ),
        in_specs=[anywhere] * 7,
        out_specs=(vmem, vmem, vmem),
        scratch_shapes=[
            pltpu.VMEM((32, 2, 32, 128), BF16),
            pltpu.VMEM((32, 2, 32, 128), jnp.int32),
            pltpu.VMEM((32, 2, 32, 128), jnp.int32),
            pltpu.VMEM((3, 4, 64, 128), BF16),
            pltpu.VMEM((32, 27, 3), BF16),
            pltpu.VMEM((32, 27, 32), BF16),
            pltpu.VMEM((1, 128), F32),
            pltpu.VMEM((4, 34, 32, 128), BF16),
            pltpu.VMEM((2, 32, 32, 128), F32),
            pltpu.VMEM((4, 64, 16, 128), BF16),
            pltpu.VMEM((4, 2, 96, 1024), BF16),
            pltpu.VMEM((2, 36, 32, 128), BF16),
            pltpu.VMEM((2, 32, 32, 128), F32),
            pltpu.VMEM((288, 96), F32),
            pltpu.VMEM((32, 144), F32),
            pltpu.VMEM((64, 192), F32),
            pltpu.VMEM((192, 192), BF16),
            pltpu.VMEM((192, 192), BF16),
            pltpu.VMEM((96, 192), F32),
            pltpu.VMEM((384, 128), F32),
            pltpu.VMEM((384, 128), F32),
            pltpu.VMEM((64, 128), F32),
            pltpu.VMEM((4, 34, 8, 128), F32),
            pltpu.VMEM((2, 3, 32, 128), F32),
            pltpu.VMEM((2, 3, 32, 128), F32),
            pltpu.VMEM((2, 2, 8, 128), F32),
            pltpu.VMEM((4, 8, 128), F32),
            pltpu.VMEM((32, 9, 128), F32),
            pltpu.VMEM((nx, 9, 128), F32),
            pltpu.VMEM((9, 128), F32),
            pltpu.VMEM((ny, 9, 128), F32),
            dma((7,)),
            dma((8,)),
            dma((8,)),
            dma((8,)),
            dma((8,)),
            dma((8,)),
            dma((8,)),
            dma((nx,)),
            dma((nx,)),
            dma((ny,)),
            dma((ny,)),
        ],
        compiler_params=pltpu.CompilerParams(
            collective_id=0, has_side_effects=True, vmem_limit_bytes=40 * 1024 * 1024
        ),
    )(cotangent, mask_first, mask_second, field_in, conv_first, conv_second, bias_row)
    return input_grad, grad_first, grad_second


def solution(mesh):
    cells = P(None, "gx", "gy", None)
    return jax.shard_map(
        functools.partial(on_device, mesh.shape["gx"], mesh.shape["gy"]),
        mesh=mesh,
        in_specs=(cells, P(), P(), P(), cells, cells, cells),
        out_specs=(cells, P("gx", None, None), P("gx", None, None)),
        check_vma=False,
    )
```

time: 54.3 us -> 45.3 us (0.83)
  Pallas kernels: 46.3 us -> 37.2 us
    pallas_call x1, Pallas kernels: 46.3 us -> 37.2 us  [on_device(): pl.pallas_call(functools.partial(kernel, nx, ny, scale), out_shape=(jax.S...]
    reshape x10 -> x0, local copies, waits for them, and re-layouts: 3.03 us -> none  [the longest x1 1.27 us: weight_forms(): second = conv_second.reshape(32, 3, 3, 3, 32)]
    unnamed x12 -> x11, local copies, waits for them, and re-layouts: 2.34 us -> 5.21 us
    pallas_call x0 -> x2, local copies, waits for them, and re-layouts: none -> 1.26 us  [on_device(): pl.pallas_call(functools.partial(kernel, nx, ny, scale), out_shape=(jax.S...]
    pad x1, local copies, waits for them, and re-layouts: 0.01 us -> 0.72 us  [on_device(): bias_row = jnp.pad(bias_first.reshape(1, 32), ((0, 0), (0, 96)))]
    rev x2 -> x0, local copies, waits for them, and re-layouts: 0.69 us -> none  [the longest x1 0.68 us: weight_forms(): w2 = second[:, ::-1, ::-1].transpose(3, 4, 1, 2, 0).reshape(96, 288)]
where the time goes in v2:
time: 45.3 us; the launch traced here: 45.1 us
  Pallas kernels  37.2 us (82%)
  local copies, waits for them, and re-layouts  7.19 us (16%)
  between operations  0.68 us (2%)
    pallas_call x1, Pallas kernels, on_device(): pl.pallas_call(functools.partial(kernel, nx, ny, scale), out_shape=(jax.S...  37.2 us
    unnamed x11, local copies, waits for them, and re-layouts  5.21 us
    pallas_call x2, local copies, waits for them, and re-layouts, on_device(): pl.pallas_call(functools.partial(kernel, nx, ny, scale), out_shape=(jax.S...  1.26 us

profile of v2, /device:TPU:1, one launch (start us, length us, event | category | flops | bytes accessed | tf_op | source)
XLA Modules:
  0.0 45.1 jit_solution(3419001755761398012)
XLA Ops:
  0.6 0.0 copy-start.2
  0.6 0.7 %pad.4.bias_in = f32[1,128]{1,0:T(1,128)S(1)} pad(f32[1,32]{1,0:T(1,128)} %bitcast.1, f32[]{:T(128)} %constant.2.clone.1), padding=0_0x0_96 | pad | bytes 644 | tf_op jit(solution)/shard_map/jit(_pad)/pad | solution.py:365
  1.4 1.1 %copy.10.first_in = bf16[32,27,3]{2,1,0:T(8,128)(2,1)S(1)} copy(bf16[32,27,3]{1,0,2:T(8,128)(2,1)} %param.8) | data formatting | bytes 10368 | tf_op args[1]
  2.4 0.0 copy-start.3
  2.4 1.0 %copy.11.second_in = bf16[32,27,32]{2,1,0:T(8,128)(2,1)S(1)} copy(bf16[32,27,32]{2,0,1:T(8,128)(2,1)} %param.10) | data formatting | bytes 110592 | tf_op args[3]
  3.5 0.0 copy-done.2
  3.5 0.0 copy-done.3
  3.5 0.0 copy-start
  3.5 1.2 %copy-done = s32[32,2,32,128]{3,2,1,0:T(8,128)S(1)} copy-done((s32[32,2,32,128]{3,2,1,0:T(8,128)S(1)}, s32[32,2,32,128]{3,2,1,0:T(8,128)}, u32[]{:S(2)}) %copy-start) | copy-done | bytes 1048600
  4.7 0.0 copy-start.1
  4.7 1.2 %copy-done.1 = s32[32,2,32,128]{3,2,1,0:T(8,128)S(1)} copy-done((s32[32,2,32,128]{3,2,1,0:T(8,128)S(1)}, s32[32,2,32,128]{3,2,1,0:T(8,128)}, u32[]{:S(2)}) %copy-start.1) | copy-done | bytes 1048600
  6.0 37.2 %shard_map.94 = (f32[3,2,32,128]{3,2,1,0:T(8,128)S(1)}, f32[1,27,3]{2,1,0:T(8,128)S(1)}, f32[1,27,32]{2,1,0:T(8,128)S(1)}) custom-call(bf16[32,2,32,128]{3,2,1,0:T(8,128)(2,1)S(1)} %copy-done.2, s32[32,2,32,128]{3,2,1,0:T(8,128)S(1)} %copy-done, s32[32,2,32,128]{3,2,1,0:T(8,128)S(1)} %copy-done.1, bf16[3,2,32,128]{3,2,1,0:T(8,128)(2,1)S(1)} %copy-done.3, ...), custom_call_target="tpu_custom_call" | custom-call | tf_op jit(solution)/shard_map/pallas_call | solution.py:369
  43.2 0.6 %copy.12 = f32[1,27,3]{1,0,2:T(1,128)} copy(f32[1,27,3]{2,1,0:T(8,128)S(1)} %get-tuple-element.4) | data formatting | bytes 648 | tf_op jit(solution)/shard_map/pallas_call | solution.py:369
  43.8 0.6 %copy.13 = f32[1,27,32]{2,0,1:T(1,128)} copy(f32[1,27,32]{2,1,0:T(8,128)S(1)} %get-tuple-element.5) | data formatting | bytes 6912 | tf_op jit(solution)/shard_map/pallas_call | solution.py:369
  44.4 0.6 %copy.15 = f32[3,2,32,128]{3,2,1,0:T(8,128)} copy(f32[3,2,32,128]{3,2,1,0:T(8,128)S(1)} %get-tuple-element.9) | data formatting | bytes 196608
Async XLA Ops:
  0.6 2.9 %copy-start.2 = (bf16[32,2,32,128]{3,2,1,0:T(8,128)(2,1)S(1)}, bf16[32,2,32,128]{3,2,1,0:T(8,128)(2,1)}, u32[]{:S(2)}) copy-start(bf16[32,2,32,128]{3,2,1,0:T(8,128)(2,1)} %cot_in.1) | copy-start | bytes 1572868
  2.4 1.1 %copy-start.3 = (bf16[3,2,32,128]{3,2,1,0:T(8,128)(2,1)S(1)}, bf16[3,2,32,128]{3,2,1,0:T(8,128)(2,1)}, u32[]{:S(2)}) copy-start(bf16[3,2,32,128]{3,2,1,0:T(8,128)(2,1)} %field_in.1) | copy-start | bytes 147460
  3.5 1.2 %copy-start = (s32[32,2,32,128]{3,2,1,0:T(8,128)S(1)}, s32[32,2,32,128]{3,2,1,0:T(8,128)}, u32[]{:S(2)}) copy-start(s32[32,2,32,128]{3,2,1,0:T(8,128)} %mask1_in.1) | copy-start | bytes 3145732
  4.7 1.2 %copy-start.1 = (s32[32,2,32,128]{3,2,1,0:T(8,128)S(1)}, s32[32,2,32,128]{3,2,1,0:T(8,128)}, u32[]{:S(2)}) copy-start(s32[32,2,32,128]{3,2,1,0:T(8,128)} %mask2_in.1) | copy-start | bytes 3145732

commit v3 on v2

--- a/solution.py
+++ b/solution.py
@@ -134,16 +134,17 @@
     form3[...] = jnp.zeros_like(form3)
     turn2[...] = jnp.zeros_like(turn2)
     turn3[...] = jnp.zeros_like(turn3)
-    taps1 = jnp.swapaxes(first_raw[...].astype(F32), 0, 1)
-    taps2 = jnp.swapaxes(second_raw[...].astype(F32), 0, 1)
     for q in range(9):
         dx, dy = q // 3, q % 3
         back2 = 32 * (8 - q)
         back3 = 32 * (3 * dx + 2 - dy)
         for dz in range(3):
-            form1[0:32, 16 * q + 3 * dz : 16 * q + 3 * dz + 3] = taps1[3 * q + dz]
-            turn2[back2 : back2 + 32, 32 * dz : 32 * dz + 32] = taps2[3 * q + dz]
-            turn3[back3 : back3 + 32, 8 * dz : 8 * dz + 3] = taps1[3 * q + dz]
+            turn2[back2 : back2 + 32, 32 * dz : 32 * dz + 32] = second_raw[3 * q + dz].astype(F32)
+        for channel in range(3):
+            taps = first_raw[channel].astype(F32)[:, 3 * q : 3 * q + 3]
+            form1[0:32, 16 * q + 3 * channel : 16 * q + 3 * channel + 3] = taps
+            for dz in range(3):
+                turn3[back3 : back3 + 32, 8 * dz + channel : 8 * dz + channel + 1] = taps[:, dz : dz + 1]
     form1[32:64, 48:192] = form1[0:32, 0:144]
     whole2 = jnp.transpose(turn2[...])[0:96].astype(BF16)
     form2[0:96, 0:192] = whole2[:, 96:288]
@@ -155,9 +156,9 @@
         for x in range(2):
             if 0 <= plane - x < 3:
                 form3[24 * plane : 24 * plane + 24, 96 * x : 96 * x + 96] = whole3[:, 96 * (plane - x) : 96 * (plane - x) + 96]
-    across = jnp.transpose(jnp.broadcast_to(bias_raw[...], (8, 128)))[0:32, 0:1]
-    bias[0:32] = jnp.broadcast_to(across, (32, 128))
-    bias[32:64] = jnp.broadcast_to(across, (32, 128))
+    bias[...] = jnp.zeros_like(bias)
+    bias[0:8, 0:32] = jnp.broadcast_to(bias_raw[...], (8, 32))
+    bias[...] = jnp.broadcast_to(jnp.transpose(bias[0:8])[0:32, 0:1], (32, 128))
 
     loads[3].wait()
     for x in range(2):
@@ -196,8 +197,8 @@
     def spread(plane, _):
         for block in range(4):
             rows = []
-            for dz in range(3):
-                for channel in range(3):
+            for channel in range(3):
+                for dz in range(3):
                     row = field_raw[channel, plane, 16 * block : 16 * block + 16, :].astype(F32)
                     rows.append(shift(row, 1 - dz))
             rows.extend([jnp.zeros((16, 128), F32)] * 7)
@@ -211,7 +212,7 @@
         pre = jnp.dot(form1_now, beside(pad_field, range(4), 8 * i + 15, 8), preferred_element_type=F32)
         for x in range(2):
             for side in range(8):
-                act = pre[32 * x : 32 * x + 32, 128 * side : 128 * side + 128] + bias[0:32]
+                act = pre[32 * x : 32 * x + 32, 128 * side : 128 * side + 128] + bias[...]
                 act = jnp.where(act >= 0, act, SLOPE * act).astype(BF16).astype(F32)
                 for tap in range(3):
                     hid3[i, x, 32 * tap : 32 * tap + 32, 128 * side : 128 * side + 128] = shift(act, 1 - tap).astype(BF16)
@@ -348,9 +349,9 @@
     total = lax.fori_loop(1, ny, take_sum, row_sum[...]) * scale
     for q in range(9):
         for dz in range(3):
-            row = slice(3 * q + dz, 3 * q + dz + 1)
-            second_out[0, row] = total[q : q + 1, 32 * dz : 32 * dz + 32]
-            first_out[0, row] = total[q : q + 1, 96 + 3 * dz : 96 + 3 * dz + 3]
+            second_out[3 * q + dz] = total[q : q + 1, 32 * dz : 32 * dz + 32]
+        for channel in range(3):
+            first_out[channel, :, 3 * q : 3 * q + 3] = total[q : q + 1, 96 + 3 * channel : 96 + 3 * channel + 3]
 
     def sent_sum(k, _):
         to = lax.rem(gy + k, ny)
@@ -360,29 +361,39 @@
     lax.fori_loop(1, ny, sent_sum, 0)
 
 
+def put_out(a, b, c, a_out, b_out, c_out, sem):
+    copies = [
+        pltpu.make_async_copy(src, dst, sem.at[i]) for i, (src, dst) in enumerate(((a, a_out), (b, b_out), (c, c_out)))
+    ]
+    for copy in copies:
+        copy.start()
+    for copy in copies:
+        copy.wait()
+
+
 def on_device(nx, ny, field_in, conv_first, bias_first, conv_second, cotangent, mask_first, mask_second):
     scale = 1.0 / math.sqrt(2 * nx * 32 * ny * 128)
-    bias_row = jnp.pad(bias_first.reshape(1, 32), ((0, 0), (0, 96)))
+    outside = pl.BlockSpec(memory_space=pltpu.HBM)
     anywhere = pl.BlockSpec(memory_space=pl.ANY)
     vmem = pl.BlockSpec(memory_space=pltpu.VMEM)
     dma = pltpu.SemaphoreType.DMA
-    input_grad, grad_first, grad_second = pl.pallas_call(
+    results = pl.pallas_call(
         functools.partial(kernel, nx, ny, scale),
         out_shape=(
             jax.ShapeDtypeStruct((3, 2, 32, 128), F32),
-            jax.ShapeDtypeStruct((1, 27, 3), F32),
-            jax.ShapeDtypeStruct((1, 27, 32), F32),
+            jax.ShapeDtypeStruct((3, 1, 27), F32),
+            jax.ShapeDtypeStruct((27, 1, 32), F32),
         ),
-        in_specs=[anywhere] * 7,
+        in_specs=[outside] * 7,
         out_specs=(vmem, vmem, vmem),
         scratch_shapes=[
             pltpu.VMEM((32, 2, 32, 128), BF16),
             pltpu.VMEM((32, 2, 32, 128), jnp.int32),
             pltpu.VMEM((32, 2, 32, 128), jnp.int32),
             pltpu.VMEM((3, 4, 64, 128), BF16),
-            pltpu.VMEM((32, 27, 3), BF16),
-            pltpu.VMEM((32, 27, 32), BF16),
-            pltpu.VMEM((1, 128), F32),
+            pltpu.VMEM((3, 32, 27), BF16),
+            pltpu.VMEM((27, 32, 32), BF16),
+            pltpu.VMEM((1, 32), F32),
             pltpu.VMEM((4, 34, 32, 128), BF16),
             pltpu.VMEM((2, 32, 32, 128), F32),
             pltpu.VMEM((4, 64, 16, 128), BF16),
@@ -397,7 +408,7 @@
             pltpu.VMEM((96, 192), F32),
             pltpu.VMEM((384, 128), F32),
             pltpu.VMEM((384, 128), F32),
-            pltpu.VMEM((64, 128), F32),
+            pltpu.VMEM((32, 128), F32),
             pltpu.VMEM((4, 34, 8, 128), F32),
             pltpu.VMEM((2, 3, 32, 128), F32),
             pltpu.VMEM((2, 3, 32, 128), F32),
@@ -420,10 +431,20 @@
             dma((ny,)),
         ],
         compiler_params=pltpu.CompilerParams(
-            collective_id=0, has_side_effects=True, vmem_limit_bytes=40 * 1024 * 1024
+            collective_id=0, has_side_effects=True, vmem_limit_bytes=60 * 1024 * 1024
         ),
-    )(cotangent, mask_first, mask_second, field_in, conv_first, conv_second, bias_row)
-    return input_grad, grad_first, grad_second
+    )(
+        cotangent, mask_first, mask_second, field_in,
+        conv_first.transpose(2, 0, 1), conv_second.transpose(1, 0, 2), bias_first.reshape(1, 32),
+    )
+    input_grad, grad_first, grad_second = pl.pallas_call(
+        put_out,
+        out_shape=tuple(jax.ShapeDtypeStruct(r.shape, r.dtype) for r in results),
+        in_specs=[anywhere] * 3,
+        out_specs=(outside,) * 3,
+        scratch_shapes=[dma((3,))],
+    )(*results)
+    return input_grad, grad_first.transpose(1, 2, 0), grad_second.transpose(1, 0, 2)
 
 
 def solution(mesh):

time: 45.3 us -> 43 us (0.949)
  local copies, waits for them, and re-layouts: 7.19 us -> 0 us
  Pallas kernels: 37.2 us -> 42.3 us
    unnamed x11 -> x0, local copies, waits for them, and re-layouts: 5.21 us -> none
    pallas_call x0 -> x1, Pallas kernels: none -> 4.57 us  [on_device(): pl.pallas_call(put_out, out_shape=tuple((jax.ShapeDtypeStruct(r.shape, r....]
    pallas_call x2 -> x0, local copies, waits for them, and re-layouts: 1.26 us -> none  [on_device(): pl.pallas_call(functools.partial(kernel, nx, ny, scale), out_shape=(jax.S...]
    pad x1 -> x0, local copies, waits for them, and re-layouts: 0.72 us -> none  [on_device(): bias_row = jnp.pad(bias_first.reshape(1, 32), ((0, 0), (0, 96)))]
    pallas_call x1, Pallas kernels: 37.2 us -> 37.7 us  [on_device(): pl.pallas_call(functools.partial(kernel, nx, ny, scale), out_shape=(jax.S...]
where the time goes in v3:
time: 43 us; the launch traced here: 42.9 us
  Pallas kernels  42.3 us (98%)
  between operations  0.64 us (1%)
    pallas_call x1, Pallas kernels, on_device(): pl.pallas_call(functools.partial(kernel, nx, ny, scale), out_shape=(jax.S...  37.7 us
    pallas_call x1, Pallas kernels, on_device(): pl.pallas_call(put_out, out_shape=tuple((jax.ShapeDtypeStruct(r.shape, r....  4.57 us

profile of v3, /device:TPU:1, one launch (start us, length us, event | category | flops | bytes accessed | tf_op | source)
XLA Modules:
  0.0 42.9 jit_solution(8570837414758990538)
XLA Ops:
  0.6 37.7 %shard_map.94 = (f32[3,2,32,128]{3,2,1,0:T(8,128)}, f32[3,1,27]{2,1,0:T(1,128)}, f32[27,1,32]{2,1,0:T(1,128)}) custom-call(bf16[32,2,32,128]{3,2,1,0:T(8,128)(2,1)} %cot_in.1, s32[32,2,32,128]{3,2,1,0:T(8,128)} %mask1_in.1, s32[32,2,32,128]{3,2,1,0:T(8,128)} %mask2_in.1, bf16[3,2,32,128]{3,2,1,0:T(8,128)(2,1)} %field_in.1, bf16[3,32,27]{2,1,0:T(8,128)(2,1)} %bitcast.6, ...), custom_call_target="tpu_custom_call" | custom-call | tf_op jit(solution)/shard_map/pallas_call | solution.py:380
  38.3 4.6 %shard_map.95 = (f32[3,2,32,128]{3,2,1,0:T(8,128)}, f32[3,1,27]{2,1,0:T(1,128)}, f32[27,1,32]{2,1,0:T(1,128)}) custom-call(f32[3,2,32,128]{3,2,1,0:T(8,128)} %get-tuple-element.9.a, f32[3,1,27]{2,1,0:T(1,128)} %get-tuple-element.10.b, f32[27,1,32]{2,1,0:T(1,128)} %get-tuple-element.11.c), custom_call_target="tpu_custom_call" | custom-call | tf_op jit(solution)/shard_map/pallas_call | solution.py:440

commit v4 on v3

--- a/solution.py
+++ b/solution.py
@@ -41,10 +41,11 @@
     cot_raw, mask1, mask2, field_raw, first_raw, second_raw, bias_raw,
     pad_cot, factors, pad_field, hid3, grad, hidden_grad, acc2, acc1,
     form1, form2, form2_far, form3, turn2, turn3, bias,
-    part, part_x, got_x, got_y, got_c, mine, got_gx, row_sum, got_gy,
-    local_sem, f_send, f_recv, p_send, p_recv, o_send, o_recv, s1_send, s1_recv, s2_send, s2_recv,
+    part, part_x, got_x, got_y, got_c, mine, got_pair, both, got_gx, row_sum, got_gy,
+    local_sem, f_send, f_recv, p_send, p_recv, o_send, o_recv, pair_sem, s1_send, s1_recv, s2_send, s2_recv,
 ):
     gx = lax.axis_index("gx")
+    core = lax.rem(gx, 2)
     gy = lax.axis_index("gy")
 
     loads = [
@@ -56,7 +57,7 @@
         pltpu.make_async_copy(second_in, second_raw, local_sem.at[5]),
         pltpu.make_async_copy(bias_in, bias_raw, local_sem.at[6]),
     ]
-    for load in loads:
+    for load in loads[0:3]:
         load.start()
 
     left, right = lax.rem(gx + nx - 1, nx), lax.rem(gx + 1, nx)
@@ -65,20 +66,22 @@
     barrier = pltpu.get_barrier_semaphore()
 
     def greet_x(k, _):
-        pl.semaphore_signal(barrier, inc=1, device_id=(lax.rem(gx + k, nx), gy), device_id_type=MESH)
+        pl.semaphore_signal(barrier, inc=1, device_id=(lax.rem(gx + 2 * k, nx), gy), device_id_type=MESH)
         return 0
 
     def greet_y(k, _):
         pl.semaphore_signal(barrier, inc=1, device_id=(gx, lax.rem(gy + k, ny)), device_id_type=MESH)
         return 0
 
-    for corner in ((left, down), (left, up), (right, down), (right, up)):
-        pl.semaphore_signal(barrier, inc=1, device_id=corner, device_id_type=MESH)
-    lax.fori_loop(1, nx, greet_x, 0)
+    for place in ((left, gy), (right, gy), (left, down), (left, up), (right, down), (right, up)):
+        pl.semaphore_signal(barrier, inc=1, device_id=place, device_id_type=MESH)
+    lax.fori_loop(1, nx // 2, greet_x, 0)
     lax.fori_loop(1, ny, greet_y, 0)
 
     loads[0].wait()
     loads[1].wait()
+    for load in loads[3:7]:
+        load.start()
     for x in range(2):
         for half in range(2):
             rows = slice(16 * half, 16 * half + 16)
@@ -86,7 +89,7 @@
             pad_cot[x + 1, 1 + 16 * half : 17 + 16 * half] = jnp.swapaxes(values, 0, 1).astype(BF16)
 
     loads[2].wait()
-    pl.semaphore_wait(barrier, (nx - 1) + (ny - 1) + 4)
+    pl.semaphore_wait(barrier, 6 + (nx // 2 - 1) + (ny - 1))
 
     def remote(src, dst, send, recv, where):
         return pltpu.make_async_remote_copy(
@@ -170,6 +173,8 @@
         for rows in (slice(0, 2), slice(34, 36)):
             grad[x, rows] = jnp.zeros((2, 32, 128), BF16)
     mine[...] = jnp.zeros_like(mine)
+    for start in (96, 224):
+        hid3[:, start : start + 32] = jnp.zeros((4, 32, 1024), BF16)
 
     def turned(out, x, side):
         total = None
@@ -215,7 +220,8 @@
                 act = pre[32 * x : 32 * x + 32, 128 * side : 128 * side + 128] + bias[...]
                 act = jnp.where(act >= 0, act, SLOPE * act).astype(BF16).astype(F32)
                 for tap in range(3):
-                    hid3[i, x, 32 * tap : 32 * tap + 32, 128 * side : 128 * side + 128] = shift(act, 1 - tap).astype(BF16)
+                    start = 128 * x + 32 * tap
+                    hid3[i, start : start + 32, 128 * side : 128 * side + 128] = shift(act, 1 - tap).astype(BF16)
         return 0
 
     lax.fori_loop(0, 4, forward, 0)
@@ -224,8 +230,7 @@
 
     def second_near(i, _):
         rows = beside(pad_cot, (1, 2), 8 * i, 8)
-        acc2[96:288] += lax.dot_general(rows, hid3[i, 0], NT, preferred_element_type=F32)
-        acc2[0:192] += lax.dot_general(rows, hid3[i, 1], NT, preferred_element_type=F32)
+        acc2[0] += lax.dot_general(rows, hid3[i], NT, preferred_element_type=F32)
         return 0
 
     lax.fori_loop(0, 4, second_near, 0)
@@ -235,8 +240,7 @@
 
     def far(i, _):
         rows = beside(pad_cot, (0, 3), 8 * i, 8)
-        acc2[0:96] += lax.dot_general(rows[0:96], hid3[i, 0], NT, preferred_element_type=F32)
-        acc2[192:288] += lax.dot_general(rows[96:192], hid3[i, 1], NT, preferred_element_type=F32)
+        acc2[1] += lax.dot_general(rows, hid3[i], NT, preferred_element_type=F32)
         out = jnp.dot(form2_far[...], rows, preferred_element_type=F32)
         for x in range(2):
             for side in range(8):
@@ -250,25 +254,39 @@
 
     def first(i, _):
         rows = beside(pad_field, range(4), 8 * i + 15, 8)
-        total = None
-        for x in range(2):
-            cells = jnp.concatenate([grad[x, 8 * i + 2 + side] for side in range(8)], axis=1)
-            term = lax.dot_general(cells, rows[48 * x : 48 * x + 144], NT, preferred_element_type=F32)
-            total = term if total is None else total + term
-        acc1[...] += total
+        cells = [
+            jnp.concatenate([grad[x, 8 * i + 2 + side] for side in range(8)], axis=1) for x in range(2)
+        ]
+        acc1[...] += lax.dot_general(jnp.concatenate(cells, axis=0), rows, NT, preferred_element_type=F32)
         return 0
 
     lax.fori_loop(0, 4, first, 0)
     for q in range(9):
-        mine[:, q, 0:96] = acc2[32 * (8 - q) : 32 * (8 - q) + 32, :]
-        mine[:, q, 96:105] = acc1[:, 16 * q : 16 * q + 9]
+        step, row = (8 - q) // 3, 32 * ((8 - q) % 3)
+        terms = []
+        for x in range(2):
+            plane = step + x
+            source, place = ((0, 96 * (plane - 1)) if plane in (1, 2) else (1, 32 * plane))
+            terms.append(acc2[source, place + row : place + row + 32, 128 * x : 128 * x + 96])
+        mine[:, :, q, 0:96] = (terms[0] + terms[1]).reshape(16, 2, 96)
+        term = acc1[0:32, 16 * q : 16 * q + 9] + acc1[32:64, 16 * q + 48 : 16 * q + 57]
+        mine[:, :, q, 96:105] = term.reshape(16, 2, 9)
+
+    other = gx + 1 - 2 * core
+    pair_copy = remote(mine.at[:, 1 - core], got_pair, pair_sem.at[0], pair_sem.at[1], (other, gy))
+    pair_copy.start()
+    pair_copy.wait_recv()
+    both[...] = mine[:, core] + got_pair[...]
+
+    def row_copy(k):
+        to = lax.rem(gx + 2 * k, nx)
+        return remote(both.at[to // 2], got_gx.at[k], s1_send.at[k], s1_recv.at[k], (to, gy))
 
     def send_row(k, _):
-        to = lax.rem(gx + k, nx)
-        remote(mine.at[to], got_gx.at[k], s1_send.at[k], s1_recv.at[k], (to, gy)).start()
-        return 0
-
-    lax.fori_loop(1, nx, send_row, 0)
+        row_copy(k).start()
+        return 0
+
+    lax.fori_loop(1, nx // 2, send_row, 0)
 
     form3_now = form3[...].astype(BF16)
 
@@ -309,11 +327,10 @@
         copy.start()
 
     def take_row(k, total):
-        to = lax.rem(gx + k, nx)
-        remote(mine.at[to], got_gx.at[k], s1_send.at[k], s1_recv.at[k], (to, gy)).wait_recv()
+        row_copy(k).wait_recv()
         return total + got_gx[k]
 
-    row_sum[...] = lax.fori_loop(1, nx, take_row, mine[gx])
+    row_sum[...] = lax.fori_loop(1, nx // 2, take_row, both[gx // 2])
 
     def send_sum(k, _):
         to = lax.rem(gy + k, ny)
@@ -333,13 +350,13 @@
         grad_out[:, x] = jnp.swapaxes(part[x + 1, 1:33], 0, 1)[0:3] + got_x[x]
 
     def sent_row(k, _):
-        to = lax.rem(gx + k, nx)
-        remote(mine.at[to], got_gx.at[k], s1_send.at[k], s1_recv.at[k], (to, gy)).wait_send()
+        row_copy(k).wait_send()
         return 0
 
     for copy in field_copies + cot_copies + part_copies:
         copy.wait_send()
-    lax.fori_loop(1, nx, sent_row, 0)
+    lax.fori_loop(1, nx // 2, sent_row, 0)
+    pair_copy.wait_send()
 
     def take_sum(k, total):
         to = lax.rem(gy + k, ny)
@@ -361,20 +378,15 @@
     lax.fori_loop(1, ny, sent_sum, 0)
 
 
-def put_out(a, b, c, a_out, b_out, c_out, sem):
-    copies = [
-        pltpu.make_async_copy(src, dst, sem.at[i]) for i, (src, dst) in enumerate(((a, a_out), (b, b_out), (c, c_out)))
-    ]
-    for copy in copies:
-        copy.start()
-    for copy in copies:
-        copy.wait()
+def put_out(a, b, c, a_out, b_out, c_out):
+    a_out[...] = a[...]
+    b_out[...] = b[...]
+    c_out[...] = c[...]
 
 
 def on_device(nx, ny, field_in, conv_first, bias_first, conv_second, cotangent, mask_first, mask_second):
     scale = 1.0 / math.sqrt(2 * nx * 32 * ny * 128)
     outside = pl.BlockSpec(memory_space=pltpu.HBM)
-    anywhere = pl.BlockSpec(memory_space=pl.ANY)
     vmem = pl.BlockSpec(memory_space=pltpu.VMEM)
     dma = pltpu.SemaphoreType.DMA
     results = pl.pallas_call(
@@ -397,11 +409,11 @@
             pltpu.VMEM((4, 34, 32, 128), BF16),
             pltpu.VMEM((2, 32, 32, 128), F32),
             pltpu.VMEM((4, 64, 16, 128), BF16),
-            pltpu.VMEM((4, 2, 96, 1024), BF16),
+            pltpu.VMEM((4, 256, 1024), BF16),
             pltpu.VMEM((2, 36, 32, 128), BF16),
             pltpu.VMEM((2, 32, 32, 128), F32),
-            pltpu.VMEM((288, 96), F32),
-            pltpu.VMEM((32, 144), F32),
+            pltpu.VMEM((2, 192, 256), F32),
+            pltpu.VMEM((64, 192), F32),
             pltpu.VMEM((64, 192), F32),
             pltpu.VMEM((192, 192), BF16),
             pltpu.VMEM((192, 192), BF16),
@@ -414,8 +426,10 @@
             pltpu.VMEM((2, 3, 32, 128), F32),
             pltpu.VMEM((2, 2, 8, 128), F32),
             pltpu.VMEM((4, 8, 128), F32),
-            pltpu.VMEM((32, 9, 128), F32),
-            pltpu.VMEM((nx, 9, 128), F32),
+            pltpu.VMEM((16, 2, 9, 128), F32),
+            pltpu.VMEM((16, 9, 128), F32),
+            pltpu.VMEM((16, 9, 128), F32),
+            pltpu.VMEM((nx // 2, 9, 128), F32),
             pltpu.VMEM((9, 128), F32),
             pltpu.VMEM((ny, 9, 128), F32),
             dma((7,)),
@@ -425,8 +439,9 @@
             dma((8,)),
             dma((8,)),
             dma((8,)),
-            dma((nx,)),
-            dma((nx,)),
+            dma((2,)),
+            dma((nx // 2,)),
+            dma((nx // 2,)),
             dma((ny,)),
             dma((ny,)),
         ],
@@ -440,9 +455,8 @@
     input_grad, grad_first, grad_second = pl.pallas_call(
         put_out,
         out_shape=tuple(jax.ShapeDtypeStruct(r.shape, r.dtype) for r in results),
-        in_specs=[anywhere] * 3,
-        out_specs=(outside,) * 3,
-        scratch_shapes=[dma((3,))],
+        in_specs=[vmem] * 3,
+        out_specs=(vmem,) * 3,
     )(*results)
     return input_grad, grad_first.transpose(1, 2, 0), grad_second.transpose(1, 0, 2)
 

time: 43 us -> 39.9 us (0.928)
  Pallas kernels: 42.3 us -> 39.1 us
    pallas_call x1, Pallas kernels: 4.57 us -> 1.56 us  [on_device(): pl.pallas_call(put_out, out_shape=tuple((jax.ShapeDtypeStruct(r.shape, r....]
where the time goes in v4:
time: 39.9 us; the launch traced here: 39.8 us
  Pallas kernels  39.1 us (98%)
  between operations  0.64 us (2%)
    pallas_call x1, Pallas kernels, on_device(): pl.pallas_call(functools.partial(kernel, nx, ny, scale), out_shape=(jax.S...  37.6 us
    pallas_call x1, Pallas kernels, on_device(): pl.pallas_call(put_out, out_shape=tuple((jax.ShapeDtypeStruct(r.shape, r....  1.56 us

profile of v4, /device:TPU:1, one launch (start us, length us, event | category | flops | bytes accessed | tf_op | source)
XLA Modules:
  0.0 39.8 jit_solution(1562337545126061727)
XLA Ops:
  0.6 37.6 %shard_map.94 = (f32[3,2,32,128]{3,2,1,0:T(8,128)}, f32[3,1,27]{2,1,0:T(1,128)}, f32[27,1,32]{2,1,0:T(1,128)}) custom-call(bf16[32,2,32,128]{3,2,1,0:T(8,128)(2,1)} %cot_in.1, s32[32,2,32,128]{3,2,1,0:T(8,128)} %mask1_in.1, s32[32,2,32,128]{3,2,1,0:T(8,128)} %mask2_in.1, bf16[3,2,32,128]{3,2,1,0:T(8,128)(2,1)} %field_in.1, bf16[3,32,27]{2,1,0:T(8,128)(2,1)} %bitcast.6, ...), custom_call_target="tpu_custom_call" | custom-call | tf_op jit(solution)/shard_map/pallas_call | solution.py:392
  38.2 1.6 %shard_map.95 = (f32[3,2,32,128]{3,2,1,0:T(8,128)}, f32[3,1,27]{2,1,0:T(1,128)}, f32[27,1,32]{2,1,0:T(1,128)}) custom-call(f32[3,2,32,128]{3,2,1,0:T(8,128)} %get-tuple-element.9.a, f32[3,1,27]{2,1,0:T(1,128)} %get-tuple-element.10.b, f32[27,1,32]{2,1,0:T(1,128)} %get-tuple-element.11.c), custom_call_target="tpu_custom_call" | custom-call | tf_op jit(solution)/shard_map/pallas_call | solution.py:455

commit v5 on v4

--- a/solution.py
+++ b/solution.py
@@ -41,11 +41,13 @@
     cot_raw, mask1, mask2, field_raw, first_raw, second_raw, bias_raw,
     pad_cot, factors, pad_field, hid3, grad, hidden_grad, acc2, acc1,
     form1, form2, form2_far, form3, turn2, turn3, bias,
-    part, part_x, got_x, got_y, got_c, mine, got_pair, both, got_gx, row_sum, got_gy,
+    part, part_x, got_x, got_y, got_c, mine, got_pair, both, got_z, two_rows, got_xy,
     local_sem, f_send, f_recv, p_send, p_recv, o_send, o_recv, pair_sem, s1_send, s1_recv, s2_send, s2_recv,
 ):
     gx = lax.axis_index("gx")
     core = lax.rem(gx, 2)
+    x_hi = lax.rem(gx // 2, 2)
+    nz = nx // 4
     gy = lax.axis_index("gy")
 
     loads = [
@@ -65,18 +67,24 @@
 
     barrier = pltpu.get_barrier_semaphore()
 
-    def greet_x(k, _):
-        pl.semaphore_signal(barrier, inc=1, device_id=(lax.rem(gx + 2 * k, nx), gy), device_id_type=MESH)
-        return 0
-
-    def greet_y(k, _):
-        pl.semaphore_signal(barrier, inc=1, device_id=(gx, lax.rem(gy + k, ny)), device_id_type=MESH)
+    def down_z(k):
+        return lax.rem(gx + 4 * k, nx)
+
+    def across(k):
+        return gx + 2 * (k // ny) * (1 - 2 * x_hi), lax.rem(gy + lax.rem(k, ny), ny)
+
+    def greet_z(k, _):
+        pl.semaphore_signal(barrier, inc=1, device_id=(down_z(k), gy), device_id_type=MESH)
+        return 0
+
+    def greet_xy(k, _):
+        pl.semaphore_signal(barrier, inc=1, device_id=across(k), device_id_type=MESH)
         return 0
 
     for place in ((left, gy), (right, gy), (left, down), (left, up), (right, down), (right, up)):
         pl.semaphore_signal(barrier, inc=1, device_id=place, device_id_type=MESH)
-    lax.fori_loop(1, nx // 2, greet_x, 0)
-    lax.fori_loop(1, ny, greet_y, 0)
+    lax.fori_loop(1, 2 * ny, greet_xy, 0)
+    lax.fori_loop(1, nz, greet_z, 0)
 
     loads[0].wait()
     loads[1].wait()
@@ -89,7 +97,7 @@
             pad_cot[x + 1, 1 + 16 * half : 17 + 16 * half] = jnp.swapaxes(values, 0, 1).astype(BF16)
 
     loads[2].wait()
-    pl.semaphore_wait(barrier, 6 + (nx // 2 - 1) + (ny - 1))
+    pl.semaphore_wait(barrier, 6 + (nz - 1) + (2 * ny - 1))
 
     def remote(src, dst, send, recv, where):
         return pltpu.make_async_remote_copy(
@@ -109,23 +117,26 @@
         (field_raw.at[:, 2:3, low], field_raw.at[:, 0:1, after]),
         (field_raw.at[:, 2:3, high], field_raw.at[:, 0:1, before]),
     ]
+    cuts = (1, 10, 18, 26, 33)
+    chunks = [slice(cuts[i], cuts[i + 1]) for i in range(4)]
     cot_moves = [
-        (pad_cot.at[1:2, 1:33], pad_cot.at[3:4, 1:33]),
-        (pad_cot.at[2:3, 1:33], pad_cot.at[0:1, 1:33]),
-        (pad_cot.at[1:3, 1:2], pad_cot.at[1:3, 33:34]),
-        (pad_cot.at[1:3, 32:33], pad_cot.at[1:3, 0:1]),
-        (pad_cot.at[1:2, 1:2], pad_cot.at[3:4, 33:34]),
-        (pad_cot.at[1:2, 32:33], pad_cot.at[3:4, 0:1]),
-        (pad_cot.at[2:3, 1:2], pad_cot.at[0:1, 33:34]),
-        (pad_cot.at[2:3, 32:33], pad_cot.at[0:1, 0:1]),
-    ]
+        (pad_cot.at[1:3, 1:2], pad_cot.at[1:3, 33:34], places[2]),
+        (pad_cot.at[1:3, 32:33], pad_cot.at[1:3, 0:1], places[3]),
+        (pad_cot.at[1:2, 1:2], pad_cot.at[3:4, 33:34], places[4]),
+        (pad_cot.at[1:2, 32:33], pad_cot.at[3:4, 0:1], places[5]),
+        (pad_cot.at[2:3, 1:2], pad_cot.at[0:1, 33:34], places[6]),
+        (pad_cot.at[2:3, 32:33], pad_cot.at[0:1, 0:1], places[7]),
+    ]
+    for chunk in chunks:
+        cot_moves.append((pad_cot.at[1:2, chunk], pad_cot.at[3:4, chunk], places[0]))
+        cot_moves.append((pad_cot.at[2:3, chunk], pad_cot.at[0:1, chunk], places[1]))
     field_copies = [
         remote(src, dst, f_send.at[i], f_recv.at[i], places[i]) for i, (src, dst) in enumerate(field_moves)
     ]
     cot_copies = [
-        remote(src, dst, p_send.at[i], p_recv.at[i], places[i]) for i, (src, dst) in enumerate(cot_moves)
-    ]
-    for copy in cot_copies[2:4] + field_copies + cot_copies[0:2] + cot_copies[4:8]:
+        remote(src, dst, p_send.at[i], p_recv.at[i], where) for i, (src, dst, where) in enumerate(cot_moves)
+    ]
+    for copy in cot_copies[0:2] + field_copies + cot_copies[2:14]:
         copy.start()
 
     loads[4].wait()
@@ -184,8 +195,8 @@
             total = term if total is None else total + term
         return total
 
-    cot_copies[2].wait_recv()
-    cot_copies[3].wait_recv()
+    cot_copies[0].wait_recv()
+    cot_copies[1].wait_recv()
 
     def backward_near(i, _):
         out = jnp.dot(form2[...], beside(pad_cot, (1, 2), 8 * i, 8), preferred_element_type=F32)
@@ -196,78 +207,64 @@
 
     lax.fori_loop(0, 4, backward_near, 0)
 
+    def spread(plane, start, count):
+        rows = []
+        for channel in range(3):
+            for dz in range(3):
+                row = field_raw[channel, plane, start : start + count, :].astype(F32)
+                rows.append(shift(row, 1 - dz))
+        rows.extend([jnp.zeros((count, 128), F32)] * 7)
+        pad_field[plane, start : start + count] = jnp.swapaxes(jnp.stack(rows, axis=0), 0, 1).astype(BF16)
+
+    for plane in (1, 2):
+        spread(plane, 16, 16)
+        spread(plane, 32, 16)
+    form1_now = form1[...].astype(BF16)
+    acc1[...] = jnp.zeros_like(acc1)
+    acc2[...] = jnp.zeros_like(acc2)
+
     for copy in field_copies:
         copy.wait_recv()
-
-    def spread(plane, _):
-        for block in range(4):
-            rows = []
-            for channel in range(3):
-                for dz in range(3):
-                    row = field_raw[channel, plane, 16 * block : 16 * block + 16, :].astype(F32)
-                    rows.append(shift(row, 1 - dz))
-            rows.extend([jnp.zeros((16, 128), F32)] * 7)
-            pad_field[plane, 16 * block : 16 * block + 16] = jnp.swapaxes(jnp.stack(rows, axis=0), 0, 1).astype(BF16)
-        return 0
-
-    lax.fori_loop(0, 4, spread, 0)
-    form1_now = form1[...].astype(BF16)
-
-    def forward(i, _):
-        pre = jnp.dot(form1_now, beside(pad_field, range(4), 8 * i + 15, 8), preferred_element_type=F32)
+    for plane in range(4):
+        spread(plane, 8, 8)
+        spread(plane, 48, 8)
+    for plane in (0, 3):
+        spread(plane, 16, 16)
+        spread(plane, 32, 16)
+
+    for copy in cot_copies[2:6]:
+        copy.wait_recv()
+    for i in range(4):
+        fields = beside(pad_field, range(4), 8 * i + 15, 8)
+        pre = jnp.dot(form1_now, fields, preferred_element_type=F32)
         for x in range(2):
             for side in range(8):
-                act = pre[32 * x : 32 * x + 32, 128 * side : 128 * side + 128] + bias[...]
+                lanes = slice(128 * side, 128 * side + 128)
+                act = pre[32 * x : 32 * x + 32, lanes] + bias[...]
                 act = jnp.where(act >= 0, act, SLOPE * act).astype(BF16).astype(F32)
                 for tap in range(3):
                     start = 128 * x + 32 * tap
-                    hid3[i, start : start + 32, 128 * side : 128 * side + 128] = shift(act, 1 - tap).astype(BF16)
-        return 0
-
-    lax.fori_loop(0, 4, forward, 0)
-
-    acc2[...] = jnp.zeros_like(acc2)
-
-    def second_near(i, _):
-        rows = beside(pad_cot, (1, 2), 8 * i, 8)
-        acc2[0] += lax.dot_general(rows, hid3[i], NT, preferred_element_type=F32)
-        return 0
-
-    lax.fori_loop(0, 4, second_near, 0)
-
-    for copy in cot_copies[0:2] + cot_copies[4:8]:
-        copy.wait_recv()
-
-    def far(i, _):
-        rows = beside(pad_cot, (0, 3), 8 * i, 8)
-        acc2[1] += lax.dot_general(rows, hid3[i], NT, preferred_element_type=F32)
-        out = jnp.dot(form2_far[...], rows, preferred_element_type=F32)
+                    hid3[i, start : start + 32, lanes] = shift(act, 1 - tap).astype(BF16)
+        for copy in cot_copies[6 + 2 * i : 8 + 2 * i]:
+            copy.wait_recv()
+        cots = beside(pad_cot, (1, 2, 0, 3), 8 * i, 8)
+        out = jnp.dot(form2_far[...], cots[192:384], preferred_element_type=F32)
         for x in range(2):
             for side in range(8):
                 total = hidden_grad[x, 8 * i + side] + turned(out, x, side)
                 grad[x, 8 * i + side + 2] = (total * factors[x, 8 * i + side]).astype(BF16)
-        return 0
-
-    lax.fori_loop(0, 4, far, 0)
-
-    acc1[...] = jnp.zeros_like(acc1)
-
-    def first(i, _):
-        rows = beside(pad_field, range(4), 8 * i + 15, 8)
+        acc2[...] += lax.dot_general(cots, hid3[i], NT, preferred_element_type=F32)
         cells = [
             jnp.concatenate([grad[x, 8 * i + 2 + side] for side in range(8)], axis=1) for x in range(2)
         ]
-        acc1[...] += lax.dot_general(jnp.concatenate(cells, axis=0), rows, NT, preferred_element_type=F32)
-        return 0
-
-    lax.fori_loop(0, 4, first, 0)
+        acc1[...] += lax.dot_general(jnp.concatenate(cells, axis=0), fields, NT, preferred_element_type=F32)
+
     for q in range(9):
         step, row = (8 - q) // 3, 32 * ((8 - q) % 3)
         terms = []
         for x in range(2):
-            plane = step + x
-            source, place = ((0, 96 * (plane - 1)) if plane in (1, 2) else (1, 32 * plane))
-            terms.append(acc2[source, place + row : place + row + 32, 128 * x : 128 * x + 96])
+            place = (192, 0, 96, 288)[step + x]
+            terms.append(acc2[place + row : place + row + 32, 128 * x : 128 * x + 96])
         mine[:, :, q, 0:96] = (terms[0] + terms[1]).reshape(16, 2, 96)
         term = acc1[0:32, 16 * q : 16 * q + 9] + acc1[32:64, 16 * q + 48 : 16 * q + 57]
         mine[:, :, q, 96:105] = term.reshape(16, 2, 9)
@@ -278,15 +275,19 @@
     pair_copy.wait_recv()
     both[...] = mine[:, core] + got_pair[...]
 
-    def row_copy(k):
-        to = lax.rem(gx + 2 * k, nx)
-        return remote(both.at[to // 2], got_gx.at[k], s1_send.at[k], s1_recv.at[k], (to, gy))
-
-    def send_row(k, _):
-        row_copy(k).start()
-        return 0
-
-    lax.fori_loop(1, nx // 2, send_row, 0)
+    def z_copy(k):
+        to = down_z(k)
+        return remote(both.at[pl.ds(2 * (to // 4), 2)], got_z.at[k], s1_send.at[k], s1_recv.at[k], (to, gy))
+
+    def xy_copy(k):
+        to = across(k)
+        return remote(two_rows.at[lax.rem(to[0] // 2, 2)], got_xy.at[k], s2_send.at[k], s2_recv.at[k], to)
+
+    def send_z(k, _):
+        z_copy(k).start()
+        return 0
+
+    lax.fori_loop(1, nz, send_z, 0)
 
     form3_now = form3[...].astype(BF16)
 
@@ -326,18 +327,17 @@
     for copy in part_copies:
         copy.start()
 
-    def take_row(k, total):
-        row_copy(k).wait_recv()
-        return total + got_gx[k]
-
-    row_sum[...] = lax.fori_loop(1, nx // 2, take_row, both[gx // 2])
-
-    def send_sum(k, _):
-        to = lax.rem(gy + k, ny)
-        remote(row_sum, got_gy.at[k], s2_send.at[k], s2_recv.at[k], (gx, to)).start()
-        return 0
-
-    lax.fori_loop(1, ny, send_sum, 0)
+    def take_z(k, total):
+        z_copy(k).wait_recv()
+        return total + got_z[k]
+
+    two_rows[...] = lax.fori_loop(1, nz, take_z, both[pl.ds(2 * (gx // 4), 2)])
+
+    def send_xy(k, _):
+        xy_copy(k).start()
+        return 0
+
+    lax.fori_loop(1, 2 * ny, send_xy, 0)
 
     for copy in part_copies:
         copy.wait_recv()
@@ -349,33 +349,31 @@
     for x in range(2):
         grad_out[:, x] = jnp.swapaxes(part[x + 1, 1:33], 0, 1)[0:3] + got_x[x]
 
-    def sent_row(k, _):
-        row_copy(k).wait_send()
+    def sent_z(k, _):
+        z_copy(k).wait_send()
         return 0
 
     for copy in field_copies + cot_copies + part_copies:
         copy.wait_send()
-    lax.fori_loop(1, nx // 2, sent_row, 0)
     pair_copy.wait_send()
-
-    def take_sum(k, total):
-        to = lax.rem(gy + k, ny)
-        remote(row_sum, got_gy.at[k], s2_send.at[k], s2_recv.at[k], (gx, to)).wait_recv()
-        return total + got_gy[k]
-
-    total = lax.fori_loop(1, ny, take_sum, row_sum[...]) * scale
+    lax.fori_loop(1, nz, sent_z, 0)
+
+    def take_xy(k, total):
+        xy_copy(k).wait_recv()
+        return total + got_xy[k]
+
+    total = lax.fori_loop(1, 2 * ny, take_xy, two_rows[x_hi]) * scale
     for q in range(9):
         for dz in range(3):
             second_out[3 * q + dz] = total[q : q + 1, 32 * dz : 32 * dz + 32]
         for channel in range(3):
             first_out[channel, :, 3 * q : 3 * q + 3] = total[q : q + 1, 96 + 3 * channel : 96 + 3 * channel + 3]
 
-    def sent_sum(k, _):
-        to = lax.rem(gy + k, ny)
-        remote(row_sum, got_gy.at[k], s2_send.at[k], s2_recv.at[k], (gx, to)).wait_send()
-        return 0
-
-    lax.fori_loop(1, ny, sent_sum, 0)
+    def sent_xy(k, _):
+        xy_copy(k).wait_send()
+        return 0
+
+    lax.fori_loop(1, 2 * ny, sent_xy, 0)
 
 
 def put_out(a, b, c, a_out, b_out, c_out):
@@ -412,7 +410,7 @@
             pltpu.VMEM((4, 256, 1024), BF16),
             pltpu.VMEM((2, 36, 32, 128), BF16),
             pltpu.VMEM((2, 32, 32, 128), F32),
-            pltpu.VMEM((2, 192, 256), F32),
+            pltpu.VMEM((384, 256), F32),
             pltpu.VMEM((64, 192), F32),
             pltpu.VMEM((64, 192), F32),
             pltpu.VMEM((192, 192), BF16),
@@ -429,21 +427,21 @@
             pltpu.VMEM((16, 2, 9, 128), F32),
             pltpu.VMEM((16, 9, 128), F32),
             pltpu.VMEM((16, 9, 128), F32),
-            pltpu.VMEM((nx // 2, 9, 128), F32),
-            pltpu.VMEM((9, 128), F32),
-            pltpu.VMEM((ny, 9, 128), F32),
+            pltpu.VMEM((nx // 4, 2, 9, 128), F32),
+            pltpu.VMEM((2, 9, 128), F32),
+            pltpu.VMEM((2 * ny, 9, 128), F32),
             dma((7,)),
             dma((8,)),
             dma((8,)),
-            dma((8,)),
-            dma((8,)),
+            dma((14,)),
+            dma((14,)),
             dma((8,)),
             dma((8,)),
             dma((2,)),
-            dma((nx // 2,)),
-            dma((nx // 2,)),
-            dma((ny,)),
-            dma((ny,)),
+            dma((nx // 4,)),
+            dma((nx // 4,)),
+            dma((2 * ny,)),
+            dma((2 * ny,)),
         ],
         compiler_params=pltpu.CompilerParams(
             collective_id=0, has_side_effects=True, vmem_limit_bytes=60 * 1024 * 1024

time: 39.9 us -> 36.7 us (0.920)
  Pallas kernels: 39.1 us -> 35.9 us
    pallas_call x1, Pallas kernels: 37.6 us -> 34.4 us  [on_device(): pl.pallas_call(functools.partial(kernel, nx, ny, scale), out_shape=(jax.S...]
where the time goes in v5:
time: 36.7 us; the launch traced here: 36.6 us
  Pallas kernels  35.9 us (98%)
  between operations  0.64 us (2%)
    pallas_call x1, Pallas kernels, on_device(): pl.pallas_call(functools.partial(kernel, nx, ny, scale), out_shape=(jax.S...  34.4 us
    pallas_call x1, Pallas kernels, on_device(): pl.pallas_call(put_out, out_shape=tuple((jax.ShapeDtypeStruct(r.shape, r....  1.56 us

profile of v5, /device:TPU:1, one launch (start us, length us, event | category | flops | bytes accessed | tf_op | source)
XLA Modules:
  0.0 36.6 jit_solution(7028014341118721)
XLA Ops:
  0.6 34.4 %shard_map.94 = (f32[3,2,32,128]{3,2,1,0:T(8,128)}, f32[3,1,27]{2,1,0:T(1,128)}, f32[27,1,32]{2,1,0:T(1,128)}) custom-call(bf16[32,2,32,128]{3,2,1,0:T(8,128)(2,1)} %cot_in.1, s32[32,2,32,128]{3,2,1,0:T(8,128)} %mask1_in.1, s32[32,2,32,128]{3,2,1,0:T(8,128)} %mask2_in.1, bf16[3,2,32,128]{3,2,1,0:T(8,128)(2,1)} %field_in.1, bf16[3,32,27]{2,1,0:T(8,128)(2,1)} %bitcast.6, ...), custom_call_target="tpu_custom_call" | custom-call | tf_op jit(solution)/shard_map/pallas_call | solution.py:390
  35.0 1.6 %shard_map.95 = (f32[3,2,32,128]{3,2,1,0:T(8,128)}, f32[3,1,27]{2,1,0:T(1,128)}, f32[27,1,32]{2,1,0:T(1,128)}) custom-call(f32[3,2,32,128]{3,2,1,0:T(8,128)} %get-tuple-element.9.a, f32[3,1,27]{2,1,0:T(1,128)} %get-tuple-element.10.b, f32[27,1,32]{2,1,0:T(1,128)} %get-tuple-element.11.c), custom_call_target="tpu_custom_call" | custom-call | tf_op jit(solution)/shard_map/pallas_call | solution.py:453

commit v6 on v5

--- a/solution.py
+++ b/solution.py
@@ -183,7 +183,6 @@
     for x in range(2):
         for rows in (slice(0, 2), slice(34, 36)):
             grad[x, rows] = jnp.zeros((2, 32, 128), BF16)
-    mine[...] = jnp.zeros_like(mine)
     for start in (96, 224):
         hid3[:, start : start + 32] = jnp.zeros((4, 32, 1024), BF16)
 
@@ -257,23 +256,27 @@
         cells = [
             jnp.concatenate([grad[x, 8 * i + 2 + side] for side in range(8)], axis=1) for x in range(2)
         ]
-        acc1[...] += lax.dot_general(jnp.concatenate(cells, axis=0), fields, NT, preferred_element_type=F32)
-
+        acc1[:, 0:192] += lax.dot_general(jnp.concatenate(cells, axis=0), fields, NT, preferred_element_type=F32)
+
+    rows = []
     for q in range(9):
         step, row = (8 - q) // 3, 32 * ((8 - q) % 3)
         terms = []
         for x in range(2):
             place = (192, 0, 96, 288)[step + x]
-            terms.append(acc2[place + row : place + row + 32, 128 * x : 128 * x + 96])
-        mine[:, :, q, 0:96] = (terms[0] + terms[1]).reshape(16, 2, 96)
-        term = acc1[0:32, 16 * q : 16 * q + 9] + acc1[32:64, 16 * q + 48 : 16 * q + 57]
-        mine[:, :, q, 96:105] = term.reshape(16, 2, 9)
+            terms.append(acc2[place + row : place + row + 32, 128 * x : 128 * x + 128])
+        rows.append(terms[0] + terms[1])
+    rows.append(acc1[0:32, 0:128] + acc1[32:64, 48:176])
+    acc1[0:32, 128:144] += acc1[32:64, 176:192]
+    rows.append(acc1[0:32, 128:256])
+    rows.extend([jnp.zeros((32, 128), F32)] * 5)
+    mine[...] = jnp.swapaxes(jnp.stack(rows, axis=0), 0, 1).reshape(16, 2, 16, 128)
 
     other = gx + 1 - 2 * core
-    pair_copy = remote(mine.at[:, 1 - core], got_pair, pair_sem.at[0], pair_sem.at[1], (other, gy))
+    pair_copy = remote(mine.at[:, 1 - core, 0:11], got_pair, pair_sem.at[0], pair_sem.at[1], (other, gy))
     pair_copy.start()
     pair_copy.wait_recv()
-    both[...] = mine[:, core] + got_pair[...]
+    both[...] = mine[:, core, 0:11] + got_pair[...]
 
     def z_copy(k):
         to = down_z(k)
@@ -367,7 +370,8 @@
         for dz in range(3):
             second_out[3 * q + dz] = total[q : q + 1, 32 * dz : 32 * dz + 32]
         for channel in range(3):
-            first_out[channel, :, 3 * q : 3 * q + 3] = total[q : q + 1, 96 + 3 * channel : 96 + 3 * channel + 3]
+            row, lane = 9 + q // 8, 16 * (q % 8) + 3 * channel
+            first_out[channel, :, 3 * q : 3 * q + 3] = total[row : row + 1, lane : lane + 3]
 
     def sent_xy(k, _):
         xy_copy(k).wait_send()
@@ -411,7 +415,7 @@
             pltpu.VMEM((2, 36, 32, 128), BF16),
             pltpu.VMEM((2, 32, 32, 128), F32),
             pltpu.VMEM((384, 256), F32),
-            pltpu.VMEM((64, 192), F32),
+            pltpu.VMEM((64, 256), F32),
             pltpu.VMEM((64, 192), F32),
             pltpu.VMEM((192, 192), BF16),
             pltpu.VMEM((192, 192), BF16),
@@ -424,12 +428,12 @@
             pltpu.VMEM((2, 3, 32, 128), F32),
             pltpu.VMEM((2, 2, 8, 128), F32),
             pltpu.VMEM((4, 8, 128), F32),
-            pltpu.VMEM((16, 2, 9, 128), F32),
-            pltpu.VMEM((16, 9, 128), F32),
-            pltpu.VMEM((16, 9, 128), F32),
-            pltpu.VMEM((nx // 4, 2, 9, 128), F32),
-            pltpu.VMEM((2, 9, 128), F32),
-            pltpu.VMEM((2 * ny, 9, 128), F32),
+            pltpu.VMEM((16, 2, 16, 128), F32),
+            pltpu.VMEM((16, 11, 128), F32),
+            pltpu.VMEM((16, 11, 128), F32),
+            pltpu.VMEM((nx // 4, 2, 11, 128), F32),
+            pltpu.VMEM((2, 11, 128), F32),
+            pltpu.VMEM((2 * ny, 11, 128), F32),
             dma((7,)),
             dma((8,)),
             dma((8,)),
@@ -444,17 +448,19 @@
             dma((2 * ny,)),
         ],
         compiler_params=pltpu.CompilerParams(
-            collective_id=0, has_side_effects=True, vmem_limit_bytes=60 * 1024 * 1024
+            collective_id=0, has_side_effects=True, vmem_limit_bytes=40 * 1024 * 1024
         ),
-    )(
+    )(*[pltpu.with_memory_space_constraint(a, pltpu.HBM) for a in (
         cotangent, mask_first, mask_second, field_in,
         conv_first.transpose(2, 0, 1), conv_second.transpose(1, 0, 2), bias_first.reshape(1, 32),
-    )
+    )])
+    results = [pltpu.with_memory_space_constraint(r, pltpu.VMEM) for r in results]
     input_grad, grad_first, grad_second = pl.pallas_call(
         put_out,
         out_shape=tuple(jax.ShapeDtypeStruct(r.shape, r.dtype) for r in results),
         in_specs=[vmem] * 3,
         out_specs=(vmem,) * 3,
+
     )(*results)
     return input_grad, grad_first.transpose(1, 2, 0), grad_second.transpose(1, 0, 2)
 

time: 36.7 us -> 35.3 us (0.962)
  Pallas kernels: 35.9 us -> 34.5 us
    pallas_call x1, Pallas kernels: 1.56 us -> 0.66 us  [on_device(): pl.pallas_call(put_out, out_shape=tuple((jax.ShapeDtypeStruct(r.shape, r....]
    pallas_call x1, Pallas kernels: 34.4 us -> 33.8 us  [on_device(): pl.pallas_call(functools.partial(kernel, nx, ny, scale), out_shape=(jax.S...]
where the time goes in v6:
time: 35.3 us; the launch traced here: 35.1 us
  Pallas kernels  34.5 us (98%)
  between operations  0.64 us (2%)
    pallas_call x1, Pallas kernels, on_device(): pl.pallas_call(functools.partial(kernel, nx, ny, scale), out_shape=(jax.S...  33.8 us

profile of v6, /device:TPU:1, one launch (start us, length us, event | category | flops | bytes accessed | tf_op | source)
XLA Modules:
  0.0 35.1 jit_solution(16374703078836345044)
XLA Ops:
  0.6 33.8 %shard_map.94 = (f32[3,2,32,128]{3,2,1,0:T(8,128)S(1)}, f32[3,1,27]{2,1,0:T(1,128)S(1)}, f32[27,1,32]{2,1,0:T(1,128)S(1)}) custom-call(bf16[32,2,32,128]{3,2,1,0:T(8,128)(2,1)} %cot_in.1, s32[32,2,32,128]{3,2,1,0:T(8,128)} %mask1_in.1, s32[32,2,32,128]{3,2,1,0:T(8,128)} %mask2_in.1, bf16[3,2,32,128]{3,2,1,0:T(8,128)(2,1)} %field_in.1, ...), custom_call_target="tpu_custom_call" | custom-call | tf_op jit(solution)/shard_map/pallas_call | solution.py:394
  34.5 0.7 %shard_map.95 = (f32[3,2,32,128]{3,2,1,0:T(8,128)}, f32[3,1,27]{2,1,0:T(1,128)}, f32[27,1,32]{2,1,0:T(1,128)}) custom-call(f32[3,2,32,128]{3,2,1,0:T(8,128)S(1)} %get-tuple-element.9.a, f32[3,1,27]{2,1,0:T(1,128)S(1)} %get-tuple-element.10.b, f32[27,1,32]{2,1,0:T(1,128)S(1)} %get-tuple-element.11.c), custom_call_target="tpu_custom_call" | custom-call | tf_op jit(solution)/shard_map/pallas_call | solution.py:458

commit v7 on v6

--- a/solution.py
+++ b/solution.py
@@ -59,32 +59,36 @@
         pltpu.make_async_copy(second_in, second_raw, local_sem.at[5]),
         pltpu.make_async_copy(bias_in, bias_raw, local_sem.at[6]),
     ]
+
+    left, right = lax.rem(gx + nx - 1, nx), lax.rem(gx + 1, nx)
+    down, up = lax.rem(gy + ny - 1, ny), lax.rem(gy + 1, ny)
+
+    barrier = pltpu.get_barrier_semaphore()
+
+    def down_z(k):
+        return lax.rem(gx + 4 * k, nx)
+
+    def across(k):
+        return gx + 2 * (k // ny) * (1 - 2 * x_hi), lax.rem(gy + lax.rem(k, ny), ny)
+
+    def greet_z(k, _):
+        far = lax.rem(k + nz // 2 - 2, nz - 1) + 1
+        pl.semaphore_signal(barrier, inc=1, device_id=(down_z(far), gy), device_id_type=MESH)
+        return 0
+
+    lax.fori_loop(1, nz, greet_z, 0)
+
+    def greet_xy(k, _):
+        pl.semaphore_signal(barrier, inc=1, device_id=across(2 * ny - k), device_id_type=MESH)
+        return 0
+
+    lax.fori_loop(1, 2 * ny, greet_xy, 0)
+
+    for place in ((left, gy), (right, gy), (left, down), (left, up), (right, down), (right, up)):
+        pl.semaphore_signal(barrier, inc=1, device_id=place, device_id_type=MESH)
+
     for load in loads[0:3]:
         load.start()
-
-    left, right = lax.rem(gx + nx - 1, nx), lax.rem(gx + 1, nx)
-    down, up = lax.rem(gy + ny - 1, ny), lax.rem(gy + 1, ny)
-
-    barrier = pltpu.get_barrier_semaphore()
-
-    def down_z(k):
-        return lax.rem(gx + 4 * k, nx)
-
-    def across(k):
-        return gx + 2 * (k // ny) * (1 - 2 * x_hi), lax.rem(gy + lax.rem(k, ny), ny)
-
-    def greet_z(k, _):
-        pl.semaphore_signal(barrier, inc=1, device_id=(down_z(k), gy), device_id_type=MESH)
-        return 0
-
-    def greet_xy(k, _):
-        pl.semaphore_signal(barrier, inc=1, device_id=across(k), device_id_type=MESH)
-        return 0
-
-    for place in ((left, gy), (right, gy), (left, down), (left, up), (right, down), (right, up)):
-        pl.semaphore_signal(barrier, inc=1, device_id=place, device_id_type=MESH)
-    lax.fori_loop(1, 2 * ny, greet_xy, 0)
-    lax.fori_loop(1, nz, greet_z, 0)
 
     loads[0].wait()
     loads[1].wait()
@@ -97,6 +101,18 @@
             pad_cot[x + 1, 1 + 16 * half : 17 + 16 * half] = jnp.swapaxes(values, 0, 1).astype(BF16)
 
     loads[2].wait()
+    def spread(plane, start, count):
+        rows = []
+        for channel in range(3):
+            for dz in range(3):
+                row = field_raw[channel, plane, start : start + count, :].astype(F32)
+                rows.append(shift(row, 1 - dz))
+        rows.extend([jnp.zeros((count, 128), F32)] * 7)
+        pad_field[plane, start : start + count] = jnp.swapaxes(jnp.stack(rows, axis=0), 0, 1).astype(BF16)
+
+    for plane in (1, 2):
+        spread(plane, 16, 16)
+        spread(plane, 32, 16)
     pl.semaphore_wait(barrier, 6 + (nz - 1) + (2 * ny - 1))
 
     def remote(src, dst, send, recv, where):
@@ -105,17 +121,16 @@
         )
 
     places = [(left, gy), (right, gy), (gx, down), (gx, up), (left, down), (left, up), (right, down), (right, up)]
-    low, high = slice(16, 32), slice(32, 48)
-    inner, before, after = slice(16, 48), slice(0, 16), slice(48, 64)
+    inner = slice(16, 48)
     field_moves = [
         (field_raw.at[:, 1:2, inner], field_raw.at[:, 3:4, inner]),
         (field_raw.at[:, 2:3, inner], field_raw.at[:, 0:1, inner]),
-        (field_raw.at[:, 1:3, low], field_raw.at[:, 1:3, after]),
-        (field_raw.at[:, 1:3, high], field_raw.at[:, 1:3, before]),
-        (field_raw.at[:, 1:2, low], field_raw.at[:, 3:4, after]),
-        (field_raw.at[:, 1:2, high], field_raw.at[:, 3:4, before]),
-        (field_raw.at[:, 2:3, low], field_raw.at[:, 0:1, after]),
-        (field_raw.at[:, 2:3, high], field_raw.at[:, 0:1, before]),
+        (pad_field.at[1:3, 16:17], pad_field.at[1:3, 48:49]),
+        (pad_field.at[1:3, 47:48], pad_field.at[1:3, 15:16]),
+        (pad_field.at[1:2, 16:17], pad_field.at[3:4, 48:49]),
+        (pad_field.at[1:2, 47:48], pad_field.at[3:4, 15:16]),
+        (pad_field.at[2:3, 16:17], pad_field.at[0:1, 48:49]),
+        (pad_field.at[2:3, 47:48], pad_field.at[0:1, 15:16]),
     ]
     cuts = (1, 10, 18, 26, 33)
     chunks = [slice(cuts[i], cuts[i + 1]) for i in range(4)]
@@ -206,27 +221,12 @@
 
     lax.fori_loop(0, 4, backward_near, 0)
 
-    def spread(plane, start, count):
-        rows = []
-        for channel in range(3):
-            for dz in range(3):
-                row = field_raw[channel, plane, start : start + count, :].astype(F32)
-                rows.append(shift(row, 1 - dz))
-        rows.extend([jnp.zeros((count, 128), F32)] * 7)
-        pad_field[plane, start : start + count] = jnp.swapaxes(jnp.stack(rows, axis=0), 0, 1).astype(BF16)
-
-    for plane in (1, 2):
-        spread(plane, 16, 16)
-        spread(plane, 32, 16)
     form1_now = form1[...].astype(BF16)
     acc1[...] = jnp.zeros_like(acc1)
     acc2[...] = jnp.zeros_like(acc2)
 
     for copy in field_copies:
         copy.wait_recv()
-    for plane in range(4):
-        spread(plane, 8, 8)
-        spread(plane, 48, 8)
     for plane in (0, 3):
         spread(plane, 16, 16)
         spread(plane, 32, 16)
@@ -287,7 +287,7 @@
         return remote(two_rows.at[lax.rem(to[0] // 2, 2)], got_xy.at[k], s2_send.at[k], s2_recv.at[k], to)
 
     def send_z(k, _):
-        z_copy(k).start()
+        z_copy(lax.rem(k + nz // 2 - 2, nz - 1) + 1).start()
         return 0
 
     lax.fori_loop(1, nz, send_z, 0)
@@ -337,7 +337,7 @@
     two_rows[...] = lax.fori_loop(1, nz, take_z, both[pl.ds(2 * (gx // 4), 2)])
 
     def send_xy(k, _):
-        xy_copy(k).start()
+        xy_copy(2 * ny - k).start()
         return 0
 
     lax.fori_loop(1, 2 * ny, send_xy, 0)

time: 35.3 us -> 34.2 us (0.969)
  Pallas kernels: 34.5 us -> 33.4 us
    pallas_call x1, Pallas kernels: 33.8 us -> 32.8 us  [on_device(): pl.pallas_call(functools.partial(kernel, nx, ny, scale), out_shape=(jax.S...]
where the time goes in v7:
time: 34.2 us; the launch traced here: 34.1 us
  Pallas kernels  33.4 us (98%)
  between operations  0.64 us (2%)
    pallas_call x1, Pallas kernels, on_device(): pl.pallas_call(functools.partial(kernel, nx, ny, scale), out_shape=(jax.S...  32.8 us

profile of v7, /device:TPU:1, one launch (start us, length us, event | category | flops | bytes accessed | tf_op | source)
XLA Modules:
  0.0 34.1 jit_solution(17937199965526989144)
XLA Ops:
  0.6 32.8 %shard_map.94 = (f32[3,2,32,128]{3,2,1,0:T(8,128)S(1)}, f32[3,1,27]{2,1,0:T(1,128)S(1)}, f32[27,1,32]{2,1,0:T(1,128)S(1)}) custom-call(bf16[32,2,32,128]{3,2,1,0:T(8,128)(2,1)} %cot_in.1, s32[32,2,32,128]{3,2,1,0:T(8,128)} %mask1_in.1, s32[32,2,32,128]{3,2,1,0:T(8,128)} %mask2_in.1, bf16[3,2,32,128]{3,2,1,0:T(8,128)(2,1)} %field_in.1, ...), custom_call_target="tpu_custom_call" | custom-call | tf_op jit(solution)/shard_map/pallas_call | solution.py:394
  33.4 0.7 %shard_map.95 = (f32[3,2,32,128]{3,2,1,0:T(8,128)}, f32[3,1,27]{2,1,0:T(1,128)}, f32[27,1,32]{2,1,0:T(1,128)}) custom-call(f32[3,2,32,128]{3,2,1,0:T(8,128)S(1)} %get-tuple-element.9.a, f32[3,1,27]{2,1,0:T(1,128)S(1)} %get-tuple-element.10.b, f32[27,1,32]{2,1,0:T(1,128)S(1)} %get-tuple-element.11.c), custom_call_target="tpu_custom_call" | custom-call | tf_op jit(solution)/shard_map/pallas_call | solution.py:458

commit v8 on v7

--- a/solution.py
+++ b/solution.py
@@ -380,10 +380,13 @@
     lax.fori_loop(1, 2 * ny, sent_xy, 0)
 
 
-def put_out(a, b, c, a_out, b_out, c_out):
-    a_out[...] = a[...]
-    b_out[...] = b[...]
-    c_out[...] = c[...]
+def put_out(a, b, c, a_out, b_out, c_out, sem):
+    pairs = ((a, a_out), (b, b_out), (c, c_out))
+    copies = [pltpu.make_async_copy(src, dst, sem.at[i]) for i, (src, dst) in enumerate(pairs)]
+    for copy in copies:
+        copy.start()
+    for copy in copies:
+        copy.wait()
 
 
 def on_device(nx, ny, field_in, conv_first, bias_first, conv_second, cotangent, mask_first, mask_second):
@@ -459,7 +462,8 @@
         put_out,
         out_shape=tuple(jax.ShapeDtypeStruct(r.shape, r.dtype) for r in results),
         in_specs=[vmem] * 3,
-        out_specs=(vmem,) * 3,
+        out_specs=(outside,) * 3,
+        scratch_shapes=[dma((3,))],
 
     )(*results)
     return input_grad, grad_first.transpose(1, 2, 0), grad_second.transpose(1, 0, 2)

time: 34.2 us -> 34.2 us (level)
  no operation moved by 1% of the time
where the time goes in v8:
time: 34.2 us; the launch traced here: 34.1 us
  Pallas kernels  33.4 us (98%)
  between operations  0.64 us (2%)
    pallas_call x1, Pallas kernels, on_device(): pl.pallas_call(functools.partial(kernel, nx, ny, scale), out_shape=(jax.S...  32.8 us

profile of v8, /device:TPU:1, one launch (start us, length us, event | category | flops | bytes accessed | tf_op | source)
XLA Modules:
  0.0 34.1 jit_solution(10375201898190071382)
XLA Ops:
  0.6 32.8 %shard_map.94 = (f32[3,2,32,128]{3,2,1,0:T(8,128)S(1)}, f32[3,1,27]{2,1,0:T(1,128)S(1)}, f32[27,1,32]{2,1,0:T(1,128)S(1)}) custom-call(bf16[32,2,32,128]{3,2,1,0:T(8,128)(2,1)} %cot_in.1, s32[32,2,32,128]{3,2,1,0:T(8,128)} %mask1_in.1, s32[32,2,32,128]{3,2,1,0:T(8,128)} %mask2_in.1, bf16[3,2,32,128]{3,2,1,0:T(8,128)(2,1)} %field_in.1, ...), custom_call_target="tpu_custom_call" | custom-call | tf_op jit(solution)/shard_map/pallas_call | solution.py:397
  33.4 0.7 %shard_map.95 = (f32[3,2,32,128]{3,2,1,0:T(8,128)}, f32[3,1,27]{2,1,0:T(1,128)}, f32[27,1,32]{2,1,0:T(1,128)}) custom-call(f32[3,2,32,128]{3,2,1,0:T(8,128)S(1)} %get-tuple-element.9.a, f32[3,1,27]{2,1,0:T(1,128)S(1)} %get-tuple-element.10.b, f32[27,1,32]{2,1,0:T(1,128)S(1)} %get-tuple-element.11.c), custom_call_target="tpu_custom_call" | custom-call | tf_op jit(solution)/shard_map/pallas_call | solution.py:461
